TPU v7x, 32 devices: a whole 2x2x4 slice. The times are simulated.
32 devices in a mesh: sec: 8 (over z, x), blk: 4 (over y, core).
Axes of the slice: x: 2, y: 2, z: 4, core: 2. Of those that a mesh axis runs over, the one named last changes fastest.
Arguments:
- features: bfloat16 [8, 52, 8192], P('sec', None, 'blk'), may hold values from -6 to 6
- programs: bfloat16 [8, 32, 8192], P('sec', None, 'blk'), may hold values from -6 to 6
- column_pot: bfloat16 [8, 8192], P('sec', 'blk'), may hold values from -12 to 12
- tile_pairs: int32 [2, 8, 112], P(None, 'sec', 'blk'), may hold values from 0 to 15, as said below
- pair_counts: int32 [8, 4], P('sec', 'blk'), may hold values from 0 to 28, as said below
Outputs:
- smoothed: bfloat16 [8, 32, 8192], P('sec', None, 'blk')
- row_potential: float32 [8, 8192], P('sec', 'blk')
- column_potential: float32 [8, 8192], P('sec', 'blk')
Inputs may be any that keep to these rules, and one draw needn't show every extreme that they name: `tile_pairs`: entry [0, s, b * 28 + k] is a row tile of block b of section s counted within the block (0 to 3); entry [1, s, b * 28 + k] is a tile of section s + 1 (0 to 15). Only slots k < pair_counts[s, b] are active; slots from there on hold in-range entries that do not count. The active pairs of one block are distinct; in every section but the last, every row tile of every block is in an active pair, and every tile of section s + 1 is in an active pair of section s. `pair_counts`: 0 in the last section; in every other section from 4 to 28, and one block of every such section holds exactly 28.
All inputs are finite; a program needn't handle non-finite values.
Results may differ from a plain program's by a relative error of at most 0.0034.
Values may be sent and summed in bfloat16 or wider, within the bound.
A program may use at most 64 MiB of HBM per device.

v0:
```python
import functools
import math

import jax
import jax.numpy as jnp
from jax import lax
from jax.experimental import pallas as pl
from jax.experimental.pallas import tpu as pltpu
from jax.sharding import PartitionSpec as P

TILE = 512
EPSILON = 0.05
LOG2E = math.log2(math.e)
LN2 = math.log(2.0)
NEG = -1e30
UNROLL = 2
SPLITS = 2
HALF = 64
EXT = 48


def split3(value):
    hi = value.astype(jnp.bfloat16).astype(jnp.float32)
    rest = value - hi
    mid = rest.astype(jnp.bfloat16).astype(jnp.float32)
    return hi, mid, rest - mid


def rows_of(pieces, width):
    index = lax.broadcasted_iota(jnp.int32, (8, width), 0)
    block = jnp.zeros((8, width), jnp.float32)
    for place, piece in enumerate(pieces):
        block = jnp.where(index == place, piece, block)
    return block


def sum_squares(cells):
    return jnp.sum(cells * cells, axis=0, keepdims=True)


def own_records(own_ref, xrec, feat, tiles_blk, tiles, bias_of):
    width = TILE // SPLITS
    gain = 2.0 * LOG2E / (feat * EPSILON)
    xrec[...] = jnp.zeros_like(xrec)

    def one(tile, carry):
        cells = own_ref[tile // tiles_blk, tile % tiles_blk].astype(jnp.float32)
        scaled = cells * gain
        high = scaled.astype(jnp.bfloat16)
        xrec[tile, 0:feat, :] = high
        xrec[tile, HALF : HALF + feat, :] = (scaled - high.astype(jnp.float32)).astype(jnp.bfloat16)
        bias = split3(bias_of(tile, cells))
        ones = jnp.ones((1, width), jnp.float32)
        aux = rows_of((ones, ones, ones) + bias, width)
        xrec[tile, HALF - 8 : HALF, :] = aux.astype(jnp.bfloat16)
        return carry

    lax.fori_loop(0, tiles, one, 0, unroll=4)


def other_records(other_ref, yrec, build, feat, tiles_blk, tiles, bias_of):
    build[...] = jnp.zeros_like(build)
    ones = jnp.ones((1, TILE), jnp.float32)

    def one(block, carry):
        for step in range(tiles_blk):
            tile, start, part = block * tiles_blk + step, step * TILE, build.at[step]
            cells = other_ref[block, 0:feat, start : start + TILE].astype(jnp.float32)
            part[0:feat, :] = cells
            part[HALF : HALF + feat, :] = cells
            bias = split3(bias_of(tile, start, cells))
            part[HALF - 8 : HALF, :] = rows_of(bias + (ones, ones, ones), TILE)
        for step in range(tiles_blk):
            tile = block * tiles_blk + step
            yrec[pl.ds(pl.multiple_of(tile * TILE, TILE), TILE), :] = build[step].T.astype(jnp.bfloat16)
        return carry

    lax.fori_loop(0, tiles // tiles_blk, one, 0)
    lane = lax.broadcasted_iota(jnp.int32, (TILE, 2 * HALF), 1)
    yrec[tiles * TILE : (tiles + 1) * TILE, :] = jnp.where(lane == HALF - 8, NEG, 0.0).astype(
        jnp.bfloat16
    )


def ext_records(prog_ref, ext, progs, tiles_blk, tiles):
    index = lax.broadcasted_iota(jnp.int32, (EXT - progs, TILE), 0)
    tail = jnp.where(index == 0, 1.0, 0.0).astype(jnp.bfloat16)

    def one(tile, carry):
        start = pl.multiple_of((tile % tiles_blk) * TILE, TILE)
        ext[tile, 0:progs, :] = prog_ref[tile // tiles_blk, :, pl.ds(start, TILE)]
        ext[tile, progs:EXT, :] = tail
        return carry

    lax.fori_loop(0, tiles, one, 0, unroll=4)
    ext[tiles] = jnp.zeros((EXT, TILE), jnp.bfloat16)


def listed_pairs(lists_ref, mine, other, most, blocks, tiles_blk, tiles, own_first, used=True):
    kinds = blocks // SPLITS
    kind = lax.axis_index("blk") // SPLITS

    def of_block(block, place):
        def one(slot, at):
            row = lists_ref[block, 0, slot] + block * tiles_blk
            col = lists_ref[block, 0, most + slot]
            held, across = (row, col) if own_first else (col, row)
            mine[at] = held // kinds
            other[at] = across
            return at + jnp.where(held % kinds == kind, 1, 0)

        return lax.fori_loop(0, jnp.where(used, lists_ref[block, 0, 2 * most], 0), one, place)

    total = lax.fori_loop(0, blocks, of_block, 0)
    last = jnp.where(total > 0, mine[jnp.maximum(total - 1, 0)], 0)
    for extra in range(2 * UNROLL):
        mine[total + extra] = last
        other[total + extra] = tiles
    return (total + UNROLL - 1) // UNROLL


def scores_of(yrec, xrec, mine, other):
    rows = yrec[pl.ds(pl.multiple_of(other * TILE, TILE), TILE), :]
    return jnp.dot(rows, xrec[mine], preferred_element_type=jnp.float32)


def over_pairs(groups, ready, tops, yrec, xrec, mine, other, use):
    def make(at, place):
        scores = scores_of(yrec, xrec, mine[at], other[at])
        ready[place][...] = scores
        if tops is not None:
            tops[place] = jnp.max(scores, axis=0, keepdims=True)

    make(0, 0)

    def group(index, carry):
        for step in range(UNROLL):
            at = index * UNROLL + step
            make(at + 1, (step + 1) % UNROLL)
            use(ready[step], None if tops is None else tops[step], mine[at], other[at])
        return carry

    lax.fori_loop(0, groups, group, 0)


def spread(parts_ref, tile, blocks, tiles_blk):
    kinds = blocks // SPLITS
    first = (tile % kinds) * SPLITS
    place = (tile % tiles_blk) // kinds
    parts = [parts_ref[first + n, tile // tiles_blk, pl.ds(place, 1), :] for n in range(SPLITS)]
    return jnp.concatenate(parts, axis=1)


def near_side(forward):
    odd = lax.axis_index("sec") % 2
    return odd if forward else 1 - odd


def lane_of(owner, place, blocks):
    kinds = blocks // SPLITS
    return (place * kinds + owner // SPLITS) * TILE + (owner % SPLITS) * (TILE // SPLITS)


def row_kernel(dims, lists_ref, own_ref, next_ref, pot_ref, rp_ref, xrec, yrec, build, high, total, mine, other, *ready):
    feat, blocks, tiles_blk, most = dims
    tiles = blocks * tiles_blk
    held_blk = tiles_blk * SPLITS // blocks
    held = blocks * held_blk
    to_score = LOG2E / EPSILON
    groups = listed_pairs(lists_ref, mine, other, most, blocks, tiles_blk, tiles, True)
    own_records(
        own_ref, xrec, feat, held_blk, held,
        lambda tile, cells: jnp.zeros((1, cells.shape[1]), jnp.float32),
    )

    def bias(tile, start, cells):
        pot = pot_ref[tile // tiles_blk, :, pl.ds(start, TILE)].astype(jnp.float32)
        return (pot - sum_squares(cells) / feat) * to_score

    other_records(next_ref.at[near_side(True)], yrec, build, feat, tiles_blk, tiles, bias)
    high[...] = jnp.full_like(high, NEG)
    total[...] = jnp.zeros_like(total)

    def use(scores_ref, top, row, col):
        old = high[row]
        new = jnp.maximum(old, jnp.max(scores_ref[...], axis=0, keepdims=True))
        part = jnp.sum(jnp.exp2(scores_ref[...] - new), axis=0, keepdims=True)
        total[row] = total[row] * jnp.exp2(old - new) + part
        high[row] = new

    over_pairs(groups, ready, None, yrec, xrec, mine, other, use)
    at_end = lax.axis_index("sec") == lax.axis_size("sec") - 1
    for tile in range(held):
        cells = own_ref[tile // held_blk, tile % held_blk].astype(jnp.float32)
        score = high[tile] + jnp.log2(total[tile]) - sum_squares(cells) * (to_score / feat)
        rp_ref[tile // held_blk, tile % held_blk : tile % held_blk + 1, :] = jnp.where(at_end, 0.0, score * (-EPSILON * LN2))


def col_kernel(dims, lists_ref, own_ref, prev_ref, rp_ref, prog_ref, cp_ref, back_ref,
               xrec, yrec, build, ext, high, total, acc, mine, other, tops, *ready):
    feat, blocks, tiles_blk, most = dims
    tiles = blocks * tiles_blk
    held_blk = tiles_blk * SPLITS // blocks
    held = blocks * held_blk
    to_score = LOG2E / EPSILON
    progs = prog_ref.shape[2]
    used = lax.axis_index("sec") > 0
    groups = listed_pairs(
        lists_ref.at[near_side(False)], mine, other, most, blocks, tiles_blk, tiles, False, used
    )
    own_records(
        own_ref, xrec, feat, held_blk, held,
        lambda tile, cells: jnp.zeros((1, cells.shape[1]), jnp.float32),
    )

    def bias(tile, start, cells):
        return (spread(rp_ref, tile, blocks, tiles_blk) - sum_squares(cells) / feat) * to_score

    other_records(prev_ref.at[near_side(False)], yrec, build, feat, tiles_blk, tiles, bias)
    ext_records(prog_ref.at[near_side(False)], ext, progs, tiles_blk, tiles)
    high[...] = jnp.full_like(high, NEG)
    total[...] = jnp.zeros_like(total)
    acc[...] = jnp.zeros_like(acc)

    def use(scores_ref, top, col, row):
        old = high[col]
        new = jnp.maximum(old, top)
        weight = jnp.exp2(scores_ref[...] - new)
        part = jnp.sum(weight, axis=0, keepdims=True)
        shrink = jnp.exp2(old - new)
        sums = jnp.dot(ext[row], weight.astype(jnp.bfloat16), preferred_element_type=jnp.float32)
        acc[col] = acc[col] * shrink + sums
        total[col] = total[col] * shrink + part
        high[col] = new

    over_pairs(groups, ready, tops, yrec, xrec, mine, other, use)
    for tile in range(held):
        cells = own_ref[tile // held_blk, tile % held_blk].astype(jnp.float32)
        filled = total[tile] > 0.0
        score = high[tile] + jnp.log2(total[tile]) - sum_squares(cells) * (to_score / feat)
        cp_ref[tile // held_blk, tile % held_blk : tile % held_blk + 1, :] = jnp.where(filled, score * (-EPSILON * LN2), 0.0)
        back_ref[tile] = jnp.where(filled, acc[tile] / total[tile], 0.0)


def plan_kernel(dims, lists_ref, own_ref, next_ref, rp_ref, cp_ref, prog_ref, back_ref, home_ref, out_ref, rows_ref, cols_ref,
                xrec, yrec, build, ext, acc, mine, other, *ready):
    feat, blocks, tiles_blk, most = dims
    tiles = blocks * tiles_blk
    held_blk = tiles_blk * SPLITS // blocks
    held = blocks * held_blk
    to_score = LOG2E / EPSILON
    progs = prog_ref.shape[2]
    groups = listed_pairs(lists_ref, mine, other, most, blocks, tiles_blk, tiles, True)
    own_records(
        own_ref, xrec, feat, held_blk, held,
        lambda tile, cells: (rp_ref[tile // held_blk, pl.ds(tile % held_blk, 1), :] - sum_squares(cells) / feat) * to_score,
    )

    def bias(tile, start, cells):
        return (spread(cp_ref, tile, blocks, tiles_blk) - sum_squares(cells) / feat) * to_score

    other_records(next_ref.at[near_side(True)], yrec, build, feat, tiles_blk, tiles, bias)
    ext_records(prog_ref.at[near_side(True)], ext, progs, tiles_blk, tiles)
    acc[...] = back_ref[...]
    width = TILE // SPLITS
    for owner in range(blocks):
        for place in range(held_blk):
            start = lane_of(owner, place, blocks)
            rows_ref[:, start : start + width] = home_ref[owner, place : place + 1, :]
            cols_ref[:, start : start + width] = cp_ref[owner, lax.axis_index("blk"), place : place + 1, :]

    def use(scores_ref, top, row, col):
        plan = jnp.exp2(scores_ref[...]).astype(jnp.bfloat16)
        acc[row] = acc[row] + jnp.dot(ext[col], plan, preferred_element_type=jnp.float32)

    over_pairs(groups, ready, None, yrec, xrec, mine, other, use)
    for tile in range(held):
        sums = acc[tile]
        out_ref[tile // held_blk, tile % held_blk] = (sums[0:progs] / sums[progs : progs + 1]).astype(jnp.bfloat16)


MESH = pl.DeviceIdType.MESH


def greet(targets):
    barrier = pltpu.get_barrier_semaphore()
    expected = jnp.int32(0)
    for used, sec, blk in targets:

        @pl.when(used)
        def _():
            pl.semaphore_signal(barrier, inc=1, device_id=(sec, blk), device_id_type=MESH)

        expected = expected + jnp.where(used, 1, 0)
    pl.semaphore_wait(barrier, expected)


def send(src, dst, sems, place, sec, blk):
    return pltpu.make_async_remote_copy(
        src_ref=src, dst_ref=dst, send_sem=sems[0].at[place], recv_sem=sems[1].at[place],
        device_id=(sec, blk), device_id_type=MESH,
    )


STAGES = 8


def gather_kernel(counts, x_ref, prog_ref, pot_ref, list_ref, own_ref, xs_ref, progs_ref, pots_ref, lists_ref,
                  all_lists_ref, send_sem, recv_sem, mate_send, mate_recv):
    n_sec, blocks = counts
    sec, blk = lax.axis_index("sec"), lax.axis_index("blk")
    even = sec % 2 == 0
    partner = jnp.where(even, sec + 1, sec - 1)
    relay_to = jnp.where(even, sec + 2, sec - 2)
    relay_from = jnp.where(even, sec - 2, sec + 2)
    has_to = jnp.logical_and(relay_to >= 0, relay_to < n_sec)
    has_from = jnp.logical_and(relay_from >= 0, relay_from < n_sec)
    core = blk + 1 - 2 * (blk % 2)
    across = (blk + 2) % blocks
    corner = core + 2 - 4 * (core // 2)
    mates = (core, across, corner)
    yes = sec >= 0
    greet(
        [(yes, partner, blk), (has_to, relay_to, blk), (has_from, relay_from, blk)]
        + [(yes, sec, mate) for mate in mates]
    )
    sems, mate_sems = (send_sem, recv_sem), (mate_send, mate_recv)
    width = TILE // SPLITS
    held_blk = x_ref.shape[1] // TILE * SPLITS // blocks
    half = x_ref.shape[1] // 2
    sources = [
        (list_ref, lists_ref, None), (x_ref, xs_ref, 0), (x_ref, xs_ref, 1), (prog_ref, progs_ref, 0), (prog_ref, progs_ref, 1),
    ]

    def cut(ref, part):
        return ref if part is None else ref.at[:, part * half : (part + 1) * half]

    def place_of(buffer, side, owner, part):
        return cut(buffer.at[side, owner], part)

    def first(c):
        src, buffer, part = sources[c]
        return send(cut(src, part), place_of(buffer, 0, blk, part), sems, STAGES * c, partner, blk)

    def relay(c):
        _, buffer, part = sources[c]
        return send(
            place_of(buffer, 0, blk, part), place_of(buffer, 1, blk, part), sems, STAGES * c + 1, relay_to, blk
        )

    def share(c, side, kind):
        _, buffer, part = sources[c]
        owner = across if kind == 2 else blk
        slot = place_of(buffer, side, owner, part)
        return send(slot, slot, sems, STAGES * c + 2 + 3 * side + kind, sec, across if kind == 0 else core)

    def to_mate(k):
        mate = mates[k]
        copies = []
        for tile in range(held_blk):
            start = pl.multiple_of(lane_of(mate, tile, blocks), width)
            copies.append((x_ref.at[:, pl.ds(start, width)], own_ref.at[blk, tile]))
        copies.append((pot_ref, pots_ref.at[blk]))
        copies.append((list_ref, all_lists_ref.at[blk]))
        per = len(copies)
        return [send(src, dst, mate_sems, per * k + n, sec, mate) for n, (src, dst) in enumerate(copies)]

    chunks = range(len(sources))
    for c in chunks:
        first(c).start()
    for k in range(3):
        for copy in to_mate(k):
            copy.start()
    for tile in range(held_blk):
        start = pl.multiple_of(lane_of(blk, tile, blocks), width)
        own_ref[blk, tile] = x_ref[:, pl.ds(start, width)]
    pots_ref[blk] = pot_ref[...]
    all_lists_ref[blk] = list_ref[...]
    for turn in range(len(sources) + 2):
        if turn in chunks:
            first(turn).wait_recv()

            @pl.when(has_to)
            def _():
                relay(turn).start()

            share(turn, 0, 0).start()
            share(turn, 0, 1).start()
        if turn - 1 in chunks:
            share(turn - 1, 0, 0).wait_recv()
            share(turn - 1, 0, 2).start()

            @pl.when(has_from)
            def _():
                relay(turn - 1).wait_recv()
                share(turn - 1, 1, 0).start()
                share(turn - 1, 1, 1).start()

        if turn - 2 in chunks:

            @pl.when(has_from)
            def _():
                share(turn - 2, 1, 0).wait_recv()
                share(turn - 2, 1, 2).start()

    for c in chunks:
        for kind in (1, 2):
            share(c, 0, kind).wait_recv()

    @pl.when(has_from)
    def _():
        for c in chunks:
            for kind in (1, 2):
                share(c, 1, kind).wait_recv()

    for k in range(3):
        for copy in to_mate(k):
            copy.wait_recv()
    for c in chunks:
        first(c).wait_send()
        for kind in range(3):
            share(c, 0, kind).wait_send()

    @pl.when(has_to)
    def _():
        for c in chunks:
            relay(c).wait_send()

    @pl.when(has_from)
    def _():
        for c in chunks:
            for kind in range(3):
                share(c, 1, kind).wait_send()

    for k in range(3):
        for copy in to_mate(k):
            copy.wait_send()


def shift_kernel(counts, steps, home, part_ref, out_ref, *rest):
    home_ref = rest[0] if home else None
    send_sem, recv_sem = rest[-2:]
    n_sec, blocks = counts
    sec, blk = lax.axis_index("sec"), lax.axis_index("blk")
    to, source = sec + steps, sec - steps
    has_to = jnp.logical_and(to >= 0, to < n_sec)
    has_from = jnp.logical_and(source >= 0, source < n_sec)
    targets = [(blk + turn) % blocks for turn in range(blocks)]
    mates = [(sec >= 0, sec, mate) for mate in targets[1:]] if home else []
    greet(mates + [(has_to, to, mate) for mate in targets] + [(has_from, source, mate) for mate in targets])

    def copy(turn):
        return send(part_ref, out_ref.at[blk], (send_sem, recv_sem), turn, to, targets[turn])

    def homeward(turn, owner):
        src = part_ref.at[targets[turn]]
        return send(src, home_ref.at[owner], (send_sem, recv_sem), blocks + turn - 1, sec, targets[turn])

    def arrival(turn):
        slot = out_ref.at[(blk + blocks - turn) % blocks]
        return send(part_ref, slot, (send_sem, recv_sem), turn, to, targets[turn])

    @pl.when(has_to)
    def _():
        for turn in range(blocks):
            copy(turn).start()

    if home:
        for turn in range(1, blocks):
            homeward(turn, blk).start()
        home_ref[blk] = part_ref[blk]
        for turn in range(1, blocks):
            homeward(turn, (blk + blocks - turn) % blocks).wait_recv()

    @pl.when(has_from)
    def _():
        for turn in range(blocks):
            arrival(turn).wait_recv()

    @pl.when(jnp.logical_not(has_from))
    def _():
        out_ref[...] = jnp.zeros_like(out_ref)

    @pl.when(has_to)
    def _():
        for turn in range(blocks):
            copy(turn).wait_send()

    if home:
        for turn in range(1, blocks):
            homeward(turn, blk).wait_send()


def return_kernel(counts, smooth_ref, out_ref, send_sem, recv_sem):
    n_sec, blocks = counts
    sec, blk = lax.axis_index("sec"), lax.axis_index("blk")
    held_blk, width = smooth_ref.shape[1], smooth_ref.shape[3]
    mates = [(blk + turn) % blocks for turn in range(blocks)]
    greet([(sec >= 0, sec, mate) for mate in mates[1:]])

    def copies(turn, owner):
        found = []
        for place in range(held_blk):
            start = pl.multiple_of(lane_of(owner, place, blocks), width)
            src, dst = smooth_ref.at[mates[turn], place], out_ref.at[:, pl.ds(start, width)]
            found.append(send(src, dst, (send_sem, recv_sem), held_blk * (turn - 1) + place, sec, mates[turn]))
        return found

    for turn in range(1, blocks):
        for copy in copies(turn, blk):
            copy.start()
    for place in range(held_blk):
        start = pl.multiple_of(lane_of(blk, place, blocks), width)
        out_ref[:, pl.ds(start, width)] = smooth_ref[blk, place]
    for turn in range(1, blocks):
        for copy in copies(turn, (blk + blocks - turn) % blocks):
            copy.wait_recv()
    for turn in range(1, blocks):
        for copy in copies(turn, blk):
            copy.wait_send()


def in_vmem(count):
    return [pl.BlockSpec(memory_space=pltpu.VMEM)] * count


def exchange(kernel, number, out_shape, operands, scratch):
    outs = jax.tree.map(lambda _: pl.BlockSpec(memory_space=pltpu.VMEM), out_shape)
    return pl.pallas_call(
        kernel, out_shape=out_shape, in_specs=in_vmem(len(operands)), out_specs=outs, scratch_shapes=scratch,
        compiler_params=pltpu.CompilerParams(collective_id=number, has_side_effects=True),
    )(*operands)


def call(kernel, out_shape, operands, scratch):
    outs = jax.tree.map(lambda _: pl.BlockSpec(memory_space=pltpu.VMEM), out_shape)
    return pl.pallas_call(
        kernel, out_shape=out_shape,
        in_specs=[pl.BlockSpec(memory_space=pltpu.SMEM)] + in_vmem(len(operands) - 1),
        out_specs=outs, scratch_shapes=scratch,
    )(*operands)


def body(features, programs, column_pot, tile_pairs, pair_counts):
    feat, cells_blk = features.shape[1:]
    progs = programs.shape[1]
    tiles_blk = cells_blk // TILE
    most = tile_pairs.shape[2]
    blocks, n_sec = lax.axis_size("blk"), lax.axis_size("sec")
    tiles = tiles_blk * blocks
    width = TILE // SPLITS
    held_blk = tiles_blk * SPLITS // blocks
    held = blocks * held_blk
    dims = (feat, blocks, tiles_blk, most)
    counts = (n_sec, blocks)
    f32, bf16 = jnp.float32, jnp.bfloat16
    shape = jax.ShapeDtypeStruct
    long = -(-(2 * most + 1) // 128) * 128
    listed = jnp.concatenate([tile_pairs[0], tile_pairs[1], pair_counts], axis=1)
    listed = jnp.pad(listed, ((0, 0), (0, long - listed.shape[1])))
    dma = pltpu.SemaphoreType.DMA
    mate_copies = (blocks - 1) * (held_blk + 2)

    own, xs, progs_all, pot, lists_all, lists = exchange(
        functools.partial(gather_kernel, counts), 0,
        (
            shape((blocks, held_blk, feat, width), bf16),
            shape((2, blocks, feat, cells_blk), bf16),
            shape((2, blocks, progs, cells_blk), bf16),
            shape((blocks, 1, cells_blk), bf16),
            shape((2, blocks, 1, long), jnp.int32),
            shape((blocks, 1, long), jnp.int32),
        ),
        (features[0], programs[0], column_pot, listed),
        [dma((STAGES * 5,)), dma((STAGES * 5,)), dma((mate_copies,)), dma((mate_copies,))],
    )

    xrec = pltpu.VMEM((held, 2 * HALF, width), bf16)
    yrec = pltpu.VMEM(((tiles + 1) * TILE, 2 * HALF), bf16)
    build = pltpu.VMEM((tiles_blk, 2 * HALF, TILE), f32)
    ext = pltpu.VMEM((tiles + 1, EXT, TILE), bf16)
    stat = pltpu.VMEM((held, 1, width), f32)
    acc = pltpu.VMEM((held, EXT, width), f32)
    index = pltpu.SMEM((blocks * most + 2 * UNROLL,), jnp.int32)
    ready = [pltpu.VMEM((TILE, width), f32)] * UNROLL
    tops = pltpu.VMEM((UNROLL, 1, width), f32)
    pots = shape((blocks, held_blk, width), f32)
    all_pots = shape((blocks, blocks, held_blk, width), f32)
    sums = shape((held, EXT, width), f32)

    row_own = call(
        functools.partial(row_kernel, dims), pots, (lists, own, xs, pot),
        [xrec, yrec, build, stat, stat, index, index, *ready],
    )
    row_prev, row_home = exchange(
        functools.partial(shift_kernel, counts, 1, True), 1, (all_pots, pots), (row_own,),
        [dma((2 * blocks - 1,)), dma((2 * blocks - 1,))],
    )
    col_own, back = call(
        functools.partial(col_kernel, dims), (pots, sums), (lists_all, own, xs, row_prev, progs_all),
        [xrec, yrec, build, ext, stat, stat, acc, index, index, tops, *ready],
    )
    col_all = exchange(
        functools.partial(shift_kernel, counts, -1, False), 2, all_pots, (col_own,), [dma((blocks,)), dma((blocks,))]
    )
    line = shape((1, cells_blk), f32)
    smooth, row_out, col_out = call(
        functools.partial(plan_kernel, dims),
        (shape((blocks, held_blk, progs, width), bf16), line, line),
        (lists, own, xs, row_own, col_all, progs_all, back, row_home),
        [xrec, yrec, build, ext, acc, index, index, *ready],
    )
    return_copies = (blocks - 1) * held_blk
    smoothed = exchange(
        functools.partial(return_kernel, counts), 3, shape((progs, cells_blk), bf16), (smooth,),
        [dma((return_copies,)), dma((return_copies,))],
    )
    return smoothed[None], row_out, col_out


def solution(mesh):
    in_specs = (
        P("sec", None, "blk"),
        P("sec", None, "blk"),
        P("sec", "blk"),
        P(None, "sec", "blk"),
        P("sec", "blk"),
    )
    out_specs = (P("sec", None, "blk"), P("sec", "blk"), P("sec", "blk"))
    return jax.shard_map(body, mesh=mesh, in_specs=in_specs, out_specs=out_specs, check_vma=False)
```

profile of v0, /device:TPU:0, one launch (start us, length us, event | category | flops | bytes accessed | tf_op | source)
XLA Modules:
  0.0 84.8 jit_solution(3269749239675883068)
XLA Ops:
  1.3 0.7 slice_bitcast_fusion.1
  2.0 0.1 pad_add_fusion
  2.0 0.5 pad.4.list_ref
  2.5 23.5 %shard_map.76 = (bf16[4,2,52,256]{3,2,1,0:T(8,128)(2,1)}, bf16[2,4,52,2048]{3,2,1,0:T(8,128)(2,1)}, bf16[2,4,32,2048]{3,2,1,0:T(8,128)(2,1)}, bf16[4,1,2048]{2,1...) custom-call(bf16[52,2048]{1,0:T(8,128)(2,1)} %bitcast.8, bf16[32,2048]{1,0:T(8,128)(2,1)} %bitcast.9, ...), custom_call_target="tpu_custom_call" | custom-call | tf_op jit(solution)/shard_map/pallas_call | solution.py:529
  26.0 8.5 %shard_map.77.part_ref.rp_ref = f32[4,2,256]{2,1,0:T(2,128)} custom-call(s32[4,1,128]{2,1,0:T(1,128)} %get-tuple-element.16.lists_ref, bf16[4,2,52,256]{3,2,1,0:T(8,128)(2,1)} %get-tuple-element.17.own_ref, bf16[2,4,52,2048]{3,2,1,0:T(8,128)(2,1)} %get-tuple-element.18.next_ref.prev_ref, bf16[4,1,2048]{2,1,0:T(2,128)(2,1)} %get-tuple-element.19.pot_ref), custom_call_target="tpu_custom_call" | custom-call | tf_op jit(solution)/shard_map/pallas_call | solution.py:537
  34.5 13.3 %shard_map.78 = (f32[4,4,2,256]{3,2,1,0:T(2,128)}, f32[4,2,256]{2,1,0:T(2,128)}) custom-call(f32[4,2,256]{2,1,0:T(2,128)} %shard_map.77.part_ref.rp_ref), custom_call_target="tpu_custom_call" | custom-call | tf_op jit(solution)/shard_map/pallas_call | solution.py:529
  47.8 4.3 %shard_map.79 = (f32[4,2,256]{2,1,0:T(2,128)}, f32[8,48,256]{2,1,0:T(8,128)}) custom-call(s32[2,4,1,128]{3,2,1,0:T(1,128)} %get-tuple-element.20.lists_ref, bf16[4,2,52,256]{3,2,1,0:T(8,128)(2,1)} %get-tuple-element.17.own_ref, bf16[2,4,52,2048]{3,2,1,0:T(8,128)(2,1)} %get-tuple-element.18.next_ref.prev_ref, f32[4,4,2,256]{3,2,1,0:T(2,128)} %get-tuple-element.21.rp_ref, ...), custom_call_target="tpu_custom_call" | custom-call | tf_op jit(solution)/shard_map/pallas_call | solution.py:537
  52.1 15.7 %shard_map.80.cp_ref = f32[4,4,2,256]{3,2,1,0:T(2,128)} custom-call(f32[4,2,256]{2,1,0:T(2,128)} %get-tuple-element.23.part_ref), custom_call_target="tpu_custom_call" | custom-call | tf_op jit(solution)/shard_map/pallas_call | solution.py:529
  67.8 9.5 %shard_map.81 = (bf16[4,2,32,256]{3,2,1,0:T(8,128)(2,1)}, f32[1,2048]{1,0:T(1,128)}, f32[1,2048]{1,0:T(1,128)}) custom-call(s32[4,1,128]{2,1,0:T(1,128)} %get-tuple-element.16.lists_ref, bf16[4,2,52,256]{3,2,1,0:T(8,128)(2,1)} %get-tuple-element.17.own_ref, bf16[2,4,52,2048]{3,2,1,0:T(8,128)(2,1)} %get-tuple-element.18.next_ref.prev_ref, ...), custom_call_target="tpu_custom_call" | custom-call | tf_op jit(solution)/shard_map/pallas_call | solution.py:537
  77.3 5.9 %shard_map.82 = bf16[32,2048]{1,0:T(8,128)(2,1)} custom-call(bf16[4,2,32,256]{3,2,1,0:T(8,128)(2,1)} %get-tuple-element.26.smooth_ref), custom_call_target="tpu_custom_call" | custom-call | tf_op jit(solution)/shard_map/pallas_call | solution.py:529
  83.3 1.6 %copy.10 = bf16[1,32,2048]{2,1,0:T(8,128)(2,1)} copy(bf16[1,32,2048]{2,1,0:T(8,128)(2,1)} %bitcast.7) | data formatting | bytes 262144
where the time goes:
time: 84.7 us; the launch traced here: 84.8 us
  Pallas kernels  80.7 us (95%)
  local copies, waits for them, and re-layouts  2.76 us (3%)
  between operations  1.31 us (2%)
    pallas_call x4, Pallas kernels, exchange(): pl.pallas_call(kernel, out_shape=out_shape, in_specs=in_vmem(len(operands...  58.4 us
    pallas_call x3, Pallas kernels, call(): pl.pallas_call(kernel, out_shape=out_shape, in_specs=[pl.BlockSpec(memory...  22.3 us

commit v1 on v0

v1 whole, which is shorter than its diff:
```python
import functools
import math

import jax
import jax.numpy as jnp
from jax import lax
from jax.experimental import pallas as pl
from jax.experimental.pallas import tpu as pltpu
from jax.sharding import PartitionSpec as P

TILE = 512
EPSILON = 0.05
LOG2E = math.log2(math.e)
NEG = -1e30
UNROLL = 2
SPLITS = 2
WIDTH = TILE // SPLITS
LANES = 128
MESH = pl.DeviceIdType.MESH


def depth_of(feat):
    return -(-(feat + 8) // 16) * 16


def ext_of(progs):
    return -(-(progs + 1) // 16) * 16


def gain_of(feat):
    return 2.0 * LOG2E / (feat * EPSILON)


def split3(value):
    hi = value.astype(jnp.bfloat16).astype(jnp.float32)
    rest = value - hi
    mid = rest.astype(jnp.bfloat16).astype(jnp.float32)
    return hi, mid, rest - mid


def rows_of(pieces, width):
    index = lax.broadcasted_iota(jnp.int32, (8, width), 0)
    block = jnp.zeros((8, width), jnp.float32)
    for place, piece in enumerate(pieces):
        block = jnp.where(index == place, piece, block)
    return block


def sum_squares(cells):
    return jnp.sum(cells * cells, axis=0, keepdims=True)


def lane_of(owner, place, blocks):
    kinds = blocks // SPLITS
    return (place * kinds + owner // SPLITS) * TILE + (owner % SPLITS) * WIDTH


def greet(targets):
    barrier = pltpu.get_barrier_semaphore()
    expected = jnp.int32(0)
    for used, sec, blk in targets:

        @pl.when(used)
        def _():
            pl.semaphore_signal(barrier, inc=1, device_id=(sec, blk), device_id_type=MESH)

        expected = expected + jnp.where(used, 1, 0)
    pl.semaphore_wait(barrier, expected)


def send(src, dst, sems, place, sec, blk):
    return pltpu.make_async_remote_copy(
        src_ref=src, dst_ref=dst, send_sem=sems[0].at[place], recv_sem=sems[1].at[place],
        device_id=(sec, blk), device_id_type=MESH,
    )


def mates_of(blk, blocks):
    core = blk + 1 - 2 * (blk % 2)
    across = (blk + 2) % blocks
    corner = core + 2 - 4 * (core // 2)
    return core, across, corner


def ext_tail(progs, width):
    index = lax.broadcasted_iota(jnp.int32, (ext_of(progs) - progs, width), 0)
    return jnp.where(index == 0, 1.0, 0.0).astype(jnp.bfloat16)


FEAT_CHUNKS = 4
PROG_CHUNKS = 2


def gather_kernel(counts, x_ref, prog_ref, pot_ref, pair_ref, count_ref,
                  xt_ref, y_ref, sq_ref, ext_next_ref, ext_own_ref, pairs_ref, counts_ref,
                  xs, progs_all, own_x, own_p, pots, build, send_sem, recv_sem, mate_send, mate_recv):
    n_sec, blocks = counts
    sec, blk = lax.axis_index("sec"), lax.axis_index("blk")
    feat, cells_blk = x_ref.shape
    progs = prog_ref.shape[0]
    depth = depth_of(feat)
    aux = depth - 8
    tiles_blk = cells_blk // TILE
    tiles = tiles_blk * blocks
    held_blk = tiles_blk * SPLITS // blocks
    has_to, has_from = sec > 0, sec < n_sec - 1
    core, across, corner = mates = mates_of(blk, blocks)
    greet(
        [(has_to, sec - 1, blk), (has_from, sec + 1, blk)] + [(sec >= 0, sec, mate) for mate in mates]
    )
    sems, mate_sems = (send_sem, recv_sem), (mate_send, mate_recv)
    feat_step, prog_step = cells_blk // FEAT_CHUNKS, cells_blk // PROG_CHUNKS
    chunks = [(x_ref, xs, n * feat_step, feat_step) for n in range(FEAT_CHUNKS)]
    chunks += [(prog_ref, progs_all, n * prog_step, prog_step) for n in range(PROG_CHUNKS)]

    def first(c):
        src, buffer, start, size = chunks[c]
        return send(
            src.at[:, start : start + size], buffer.at[blk, :, start : start + size], sems, 4 * c, sec - 1, blk
        )

    def share(c, kind):
        _, buffer, start, size = chunks[c]
        slot = buffer.at[across if kind == 2 else blk, :, start : start + size]
        return send(slot, slot, sems, 4 * c + 1 + kind, sec, across if kind == 0 else core)

    def to_mate(k):
        mate = mates[k]
        copies = [(pot_ref, pots.at[blk]), (pair_ref, pairs_ref.at[blk]), (count_ref, counts_ref.at[blk])]
        for place in range(held_blk):
            start = pl.multiple_of(lane_of(mate, place, blocks), WIDTH)
            copies.append((x_ref.at[:, pl.ds(start, WIDTH)], own_x.at[blk, place]))
        for place in range(held_blk):
            start = pl.multiple_of(lane_of(mate, place, blocks), WIDTH)
            copies.append((prog_ref.at[:, pl.ds(start, WIDTH)], own_p.at[blk, place]))
        per = len(copies)
        return [send(src, dst, mate_sems, per * k + n, sec, mate) for n, (src, dst) in enumerate(copies)]

    @pl.when(has_to)
    def _():
        for c in range(len(chunks)):
            first(c).start()

    to_mates = [to_mate(k) for k in range(3)]
    for n in range(len(to_mates[0])):
        for k in (1, 2, 0):
            to_mates[k][n].start()

    build[...] = jnp.zeros_like(build)
    build[aux : aux + 8, :] = rows_of([1.0] * 3, WIDTH)
    row = lax.broadcasted_iota(jnp.int32, (depth, TILE), 0)
    y_ref[tiles] = jnp.where(row == aux, NEG, 0.0).astype(jnp.bfloat16)
    ext_next_ref[tiles] = jnp.zeros(ext_next_ref.shape[1:], jnp.bfloat16)
    for place in range(held_blk):
        start = pl.multiple_of(lane_of(blk, place, blocks), WIDTH)
        own_x[blk, place] = x_ref[:, pl.ds(start, WIDTH)]
        own_p[blk, place] = prog_ref[:, pl.ds(start, WIDTH)]
    pots[blk] = pot_ref[...]
    pairs_ref[blk] = pair_ref[...]
    counts_ref[blk] = count_ref[...]

    def build_own(owner):
        for place in range(held_blk):
            held = owner * held_blk + place
            cells = own_x[owner, place].astype(jnp.float32)
            build[0:feat, :] = cells
            xt_ref[held] = build[...].T.astype(jnp.bfloat16)
            sq_ref[owner, place : place + 1, :] = sum_squares(cells)
            ext_own_ref[held, 0:progs, :] = own_p[owner, place]
            ext_own_ref[held, progs:, :] = ext_tail(progs, WIDTH)

    ones = jnp.ones((1, TILE), jnp.float32)

    def build_next(owner, c):
        source, _, begin, size = chunks[c]
        for start in range(begin, begin + size, TILE):
            tile = owner * tiles_blk + start // TILE
            if source is x_ref:
                raw = xs[owner, :, start : start + TILE]
                cells = raw.astype(jnp.float32)
                pot = pots[owner, :, start : start + TILE].astype(jnp.float32)
                bias = pot * (feat / 2) - sum_squares(cells) * 0.5
                y_ref[tile, 0:feat, :] = raw
                y_ref[tile, feat:aux, :] = jnp.zeros((aux - feat, TILE), jnp.bfloat16)
                y_ref[tile, aux:depth, :] = rows_of(split3(bias) + (ones,) * 3, TILE).astype(jnp.bfloat16)
            else:
                ext_next_ref[tile, 0:progs, :] = progs_all[owner, :, start : start + TILE]
                ext_next_ref[tile, progs:, :] = ext_tail(progs, TILE)

    build_own(blk)
    for k in range(3):
        for copy in to_mates[k][:3]:
            copy.wait_recv()

    @pl.when(has_from)
    def _():
        for turn in range(len(chunks) + 2):
            if turn < len(chunks):
                first(turn).wait_recv()
                share(turn, 0).start()
                share(turn, 1).start()
                build_next(blk, turn)
            if 0 <= turn - 1 < len(chunks):
                share(turn - 1, 0).wait_recv()
                share(turn - 1, 2).start()
                build_next(across, turn - 1)
                share(turn - 1, 1).wait_recv()
                build_next(core, turn - 1)
            if 0 <= turn - 2 < len(chunks):
                share(turn - 2, 2).wait_recv()
                build_next(corner, turn - 2)

    for k, mate in enumerate(mates):
        for copy in to_mates[k][3:]:
            copy.wait_recv()
        build_own(mate)

    @pl.when(has_to)
    def _():
        for c in range(len(chunks)):
            first(c).wait_send()

    @pl.when(has_from)
    def _():
        for c in range(len(chunks)):
            for kind in range(3):
                share(c, kind).wait_send()

    for k in range(3):
        for copy in to_mates[k]:
            copy.wait_send()


def listed_pairs(pairs_ref, counts_ref, mine, other, blocks, tiles_blk, tiles):
    kinds = blocks // SPLITS
    kind = lax.axis_index("blk") // SPLITS

    def of_block(block, place):
        def one(slot, at):
            row = pairs_ref[block, 0, 0, slot] + block * tiles_blk
            mine[at] = row // kinds
            other[at] = pairs_ref[block, 1, 0, slot]
            return at + jnp.where(row % kinds == kind, 1, 0)

        return lax.fori_loop(0, counts_ref[block, 0, 0], one, place)

    total = lax.fori_loop(0, blocks, of_block, 0)
    last = jnp.where(total > 0, mine[jnp.maximum(total - 1, 0)], 0)
    for extra in range(2 * UNROLL):
        mine[total + extra] = last
        other[total + extra] = tiles
    return (total + UNROLL - 1) // UNROLL


def over_pairs(groups, ready, xt, y_ref, mine, other, use):
    def make(at, place):
        ready[place][...] = jnp.dot(xt[mine[at]], y_ref[other[at]], preferred_element_type=jnp.float32)

    make(0, 0)

    def group(index, carry):
        for step in range(UNROLL):
            at = index * UNROLL + step
            make(at + 1, (step + 1) % UNROLL)
            use(ready[step], mine[at], other[at])
        return carry

    lax.fori_loop(0, groups, group, 0)


STRIP = 64


def stats_kernel(dims, pairs_ref, counts_ref, xt_ref, y_ref, sq_ref, rp_ref, xt_out, cl_ref,
                 top_row, sum_row, top_col, sum_col, mine, other, *ready):
    feat, blocks, tiles_blk = dims
    tiles = blocks * tiles_blk
    held_blk = tiles_blk * SPLITS // blocks
    held = blocks * held_blk
    gain = gain_of(feat)
    aux = depth_of(feat) - 8
    at_end = lax.axis_index("sec") == lax.axis_size("sec") - 1
    groups = listed_pairs(pairs_ref, counts_ref, mine, other, blocks, tiles_blk, tiles)
    for ref in (top_row, top_col):
        ref[...] = jnp.full_like(ref, NEG)
    for ref in (sum_row, sum_col):
        ref[...] = jnp.zeros_like(ref)
    parts = TILE // LANES

    def row_use(scores, row, col):
        for start in range(0, WIDTH, STRIP):
            here = pl.ds(start, STRIP)
            pieces = [scores[here, n * LANES : (n + 1) * LANES] for n in range(parts)]
            old = top_row[row, here, :]
            new = functools.reduce(jnp.maximum, pieces, old)
            part = sum_row[row, here, :] * jnp.exp2((old - new) * gain)
            for piece in pieces:
                part = part + jnp.exp2((piece - new) * gain)
            sum_row[row, here, :] = part
            top_row[row, here, :] = new

    over_pairs(groups, ready, xt_ref, y_ref, mine, other, row_use)
    lane = lax.broadcasted_iota(jnp.int32, (WIDTH, LANES), 1)
    record_lane = lax.broadcasted_iota(jnp.int32, (WIDTH, xt_ref.shape[2]), 1)
    columns = jnp.zeros((WIDTH, LANES), jnp.float32)
    for row in range(held):
        tops = top_row[row]
        top = jnp.max(tops, axis=1, keepdims=True)
        total = jnp.sum(sum_row[row] * jnp.exp2((tops - top) * gain), axis=1, keepdims=True)
        level = top + jnp.log2(total) * (1.0 / gain)
        columns = jnp.where(lane == row, level, columns)
        record = xt_ref[row].astype(jnp.float32)
        for place, piece in enumerate(split3(-level)):
            record = jnp.where(record_lane == aux + 3 + place, piece, record)
        xt_out[row] = record.astype(jnp.bfloat16)
    levels = columns.T
    for row in range(held):
        owner, place = row // held_blk, row % held_blk
        potential = (sq_ref[owner, place : place + 1, :] - 2.0 * levels[row : row + 1, :]) * (1.0 / feat)
        rp_ref[owner, place : place + 1, :] = jnp.where(at_end, 0.0, potential)

    def col_use(scores, row, col):
        for n in range(parts):
            here = slice(n * LANES, (n + 1) * LANES)
            block = scores[:, here].reshape(WIDTH // 8, 8, LANES)
            old = top_col[col, :, here]
            new = jnp.maximum(old, jnp.max(block, axis=0))
            part = jnp.sum(jnp.exp2((block - new) * gain), axis=0)
            sum_col[col, :, here] = sum_col[col, :, here] * jnp.exp2((old - new) * gain) + part
            top_col[col, :, here] = new

    over_pairs(groups, ready, xt_out, y_ref, mine, other, col_use)
    for col in range(tiles):
        tops = top_col[col]
        top = jnp.max(tops, axis=0, keepdims=True)
        total = jnp.sum(sum_col[col] * jnp.exp2((tops - top) * gain), axis=0, keepdims=True)
        level = jnp.where(total > 0.0, top + jnp.log2(total) * (1.0 / gain), NEG)
        cl_ref[col : col + 1, :] = level


def merge_kernel(counts, feat, rp_ref, cl_ref, level_ref, home_ref, parts, send_sem, recv_sem):
    n_sec, blocks = counts
    sec, blk = lax.axis_index("sec"), lax.axis_index("blk")
    tiles = cl_ref.shape[0]
    gain = gain_of(feat)
    mates = mates_of(blk, blocks)
    sems = (send_sem, recv_sem)
    greet([(sec >= 0, sec, mate) for mate in mates])
    copies = []
    for k, mate in enumerate(mates):
        copies.append(send(cl_ref, parts.at[blk], sems, 2 * k, sec, mate))
        copies.append(send(rp_ref.at[mate], home_ref.at[blk], sems, 2 * k + 1, sec, mate))
    for k in (1, 2, 0):
        for copy in copies[2 * k : 2 * k + 2]:
            copy.start()
    parts[blk] = cl_ref[...]
    home_ref[blk] = rp_ref[blk]
    level_ref[tiles:, :] = jnp.zeros((level_ref.shape[0] - tiles, TILE), jnp.float32)
    for copy in copies:
        copy.wait_recv()
    levels = [parts[n] for n in range(blocks)]
    top = functools.reduce(jnp.maximum, levels)
    total = functools.reduce(jnp.add, [jnp.exp2((level - top) * gain) for level in levels])
    level_ref[0:tiles, :] = top + jnp.log2(total) * (1.0 / gain)
    for copy in copies:
        copy.wait_send()


def plan_kernel(dims, pairs_ref, counts_ref, xt_ref, y_ref, level_ref, ext_next_ref, ext_own_ref, pot_ref, home_ref,
                fnum_ref, fden_ref, bnum_ref, bden_ref, rows_ref, cols_ref, acc_row, acc_col, mine, other, *ready):
    feat, blocks, tiles_blk = dims
    tiles = blocks * tiles_blk
    held_blk = tiles_blk * SPLITS // blocks
    held = blocks * held_blk
    gain = gain_of(feat)
    progs = fnum_ref.shape[1]
    at_end = lax.axis_index("sec") == lax.axis_size("sec") - 1
    groups = listed_pairs(pairs_ref, counts_ref, mine, other, blocks, tiles_blk, tiles)
    acc_row[...] = jnp.zeros_like(acc_row)
    acc_col[...] = jnp.zeros_like(acc_col)
    for owner in range(blocks):
        for place in range(held_blk):
            start = lane_of(owner, place, blocks)
            rows_ref[:, start : start + WIDTH] = home_ref[owner, place : place + 1, :]
    blk = lax.axis_index("blk")
    for tile in range(tiles_blk):
        here = slice(tile * TILE, (tile + 1) * TILE)
        level = level_ref[pl.ds(blk * tiles_blk + tile, 1), :]
        potential = pot_ref[:, here].astype(jnp.float32) - level * (2.0 / feat)
        cols_ref[:, here] = jnp.where(at_end, 0.0, potential)

    def use(scores, row, col):
        level = level_ref[pl.ds(col, 1), :]
        plan = jnp.exp2((scores[...] - level) * gain).astype(jnp.bfloat16)
        acc_row[row] += lax.dot_general(
            ext_next_ref[col], plan, (((1,), (1,)), ((), ())), preferred_element_type=jnp.float32
        )
        acc_col[col] += jnp.dot(ext_own_ref[row], plan, preferred_element_type=jnp.float32)

    over_pairs(groups, ready, xt_ref, y_ref, mine, other, use)
    for row in range(held):
        owner, place = row // held_blk, row % held_blk
        fnum_ref[owner, :, place * WIDTH : (place + 1) * WIDTH] = acc_row[row, 0:progs, :].astype(jnp.bfloat16)
        fden_ref[owner, place : place + 1, :] = acc_row[row, progs : progs + 1, :]
    for col in range(tiles):
        owner, place = col // tiles_blk, col % tiles_blk
        bnum_ref[owner, place] = acc_col[col, 0:progs, :].astype(jnp.bfloat16)
        bden_ref[owner, place : place + 1, :] = acc_col[col, progs : progs + 1, :]


def finish_kernel(counts, fnum_ref, fden_ref, bnum_ref, bden_ref, out_ref,
                  hn, hd, an, ad, keep, keep_den, go, go_den, bn, bd, ship, ship_den, cn, cd,
                  send_sem, recv_sem):
    n_sec, blocks = counts
    sec, blk = lax.axis_index("sec"), lax.axis_index("blk")
    tiles_blk = bnum_ref.shape[1]
    held_blk = fden_ref.shape[1]
    kinds = blocks // SPLITS
    has_to, has_from = sec < n_sec - 1, sec > 0
    core, across, corner = mates = mates_of(blk, blocks)
    me, side = blk % 2, blk // 2
    sems = (send_sem, recv_sem)
    greet(
        [(has_to, sec + 1, blk), (has_from, sec - 1, blk)] + [(sec >= 0, sec, mate) for mate in mates]
    )

    def homeward(k, n):
        mate = mates[k]
        src, dst = ((fnum_ref, hn), (fden_ref, hd))[n]
        return send(src.at[mate], dst.at[blk], sems, 2 * k + n, sec, mate)

    steps = tiles_blk + 1
    base = 6

    def pair(t, far):
        place = 1 - side if far else side
        source = 2 * place + 1 - me
        number = base + 2 * t + (0 if far else 1)
        slot = 0 if far else 1
        if t == tiles_blk:
            return send(bden_ref.at[source], ad.at[slot], sems, number, sec, core)
        return send(bnum_ref.at[source, t], an.at[slot, t], sems, number, sec, core)

    def cross(t):
        number = base + 2 * steps + t
        if t == tiles_blk:
            return send(go_den, bd, sems, number, sec, across)
        return send(go.at[t], bn.at[t], sems, number, sec, across)

    def onward(t):
        number = base + 3 * steps + t
        if t == tiles_blk:
            return send(ship_den, cd, sems, number, sec + 1, blk)
        return send(ship.at[t], cn.at[t], sems, number, sec + 1, blk)

    order = [tiles_blk] + list(range(tiles_blk))

    @pl.when(has_to)
    def _():
        for t in order:
            pair(t, True).start()
        for t in order:
            pair(t, False).start()

    for k in (1, 2, 0):
        for n in range(2):
            homeward(k, n).start()
    hn[blk] = fnum_ref[blk]
    hd[blk] = fden_ref[blk]

    @pl.when(has_to)
    def _():
        far, near = 2 * (1 - side) + me, 2 * side + me
        for t in order:
            pair(t, True).wait_recv()
            if t == tiles_blk:
                go_den[...] = bden_ref[far] + ad[0]
            else:
                go[t] = (bnum_ref[far, t].astype(jnp.float32) + an[0, t].astype(jnp.float32)).astype(jnp.bfloat16)
            cross(t).start()
        for t in order:
            pair(t, False).wait_recv()
            if t == tiles_blk:
                keep_den[...] = bden_ref[near] + ad[1]
            else:
                keep[t] = bnum_ref[near, t].astype(jnp.float32) + an[1, t].astype(jnp.float32)
        for t in order:
            cross(t).wait_recv()
            if t == tiles_blk:
                ship_den[...] = keep_den[...] + bd[...]
            else:
                ship[t] = (keep[t] + bn[t].astype(jnp.float32)).astype(jnp.bfloat16)
            onward(t).start()

    for k in range(3):
        for n in range(2):
            homeward(k, n).wait_recv()

    @pl.when(jnp.logical_not(has_from))
    def _():
        cn[...] = jnp.zeros_like(cn)
        cd[...] = jnp.zeros_like(cd)

    for t in order:

        @pl.when(has_from)
        def _():
            onward(t).wait_recv()

        if t == tiles_blk:
            continue
        place, kind = t // kinds, t % kinds
        owners = [kind * SPLITS + n for n in range(SPLITS)]
        here = slice(place * WIDTH, (place + 1) * WIDTH)
        for n, owner in enumerate(owners):
            part = slice(n * WIDTH, (n + 1) * WIDTH)
            number = hn[owner, :, here].astype(jnp.float32) + cn[t, :, part].astype(jnp.float32)
            weight = hd[owner, place : place + 1, :] + cd[t : t + 1, part]
            start = t * TILE + n * WIDTH
            out_ref[:, start : start + WIDTH] = (number / weight).astype(jnp.bfloat16)

    for k in range(3):
        for n in range(2):
            homeward(k, n).wait_send()

    @pl.when(has_to)
    def _():
        for t in range(steps):
            pair(t, True).wait_send()
            pair(t, False).wait_send()
            cross(t).wait_send()
            onward(t).wait_send()


def in_vmem(count):
    return [pl.BlockSpec(memory_space=pltpu.VMEM)] * count


def exchange(kernel, number, out_shape, operands, scratch):
    outs = jax.tree.map(lambda _: pl.BlockSpec(memory_space=pltpu.VMEM), out_shape)
    return pl.pallas_call(
        kernel, out_shape=out_shape, in_specs=in_vmem(len(operands)), out_specs=outs, scratch_shapes=scratch,
        compiler_params=pltpu.CompilerParams(collective_id=number, has_side_effects=True),
    )(*operands)


def call(kernel, out_shape, operands, scratch):
    outs = jax.tree.map(lambda _: pl.BlockSpec(memory_space=pltpu.VMEM), out_shape)
    return pl.pallas_call(
        kernel, out_shape=out_shape,
        in_specs=[pl.BlockSpec(memory_space=pltpu.SMEM)] * 2 + in_vmem(len(operands) - 2),
        out_specs=outs, scratch_shapes=scratch,
    )(*operands)


def body(features, programs, column_pot, tile_pairs, pair_counts):
    feat, cells_blk = features.shape[1:]
    progs = programs.shape[1]
    tiles_blk = cells_blk // TILE
    most = tile_pairs.shape[2]
    blocks, n_sec = lax.axis_size("blk"), lax.axis_size("sec")
    tiles = tiles_blk * blocks
    held_blk = tiles_blk * SPLITS // blocks
    held = blocks * held_blk
    dims = (feat, blocks, tiles_blk)
    counts = (n_sec, blocks)
    depth, ext = depth_of(feat), ext_of(progs)
    f32, bf16, i32 = jnp.float32, jnp.bfloat16, jnp.int32
    shape, vmem = jax.ShapeDtypeStruct, pltpu.VMEM

    def dma(number):
        return [pltpu.SemaphoreType.DMA((number,))] * 2

    mate_copies = (blocks - 1) * (2 * held_blk + 3)
    xt, y, sq, ext_next, ext_own, pairs, all_counts = exchange(
        functools.partial(gather_kernel, counts), 0,
        (
            shape((held, WIDTH, depth), bf16),
            shape((tiles + 1, depth, TILE), bf16),
            shape((blocks, held_blk, WIDTH), f32),
            shape((tiles + 1, ext, TILE), bf16),
            shape((held, ext, WIDTH), bf16),
            shape((blocks, 2, 1, most), i32),
            shape((blocks, 1, 1), i32),
        ),
        (features[0], programs[0], column_pot, tile_pairs, pair_counts),
        [
            vmem((blocks, feat, cells_blk), bf16),
            vmem((blocks, progs, cells_blk), bf16),
            vmem((blocks, held_blk, feat, WIDTH), bf16),
            vmem((blocks, held_blk, progs, WIDTH), bf16),
            vmem((blocks, 1, cells_blk), bf16),
            vmem((depth, WIDTH), f32),
            *dma(4 * (FEAT_CHUNKS + PROG_CHUNKS)), *dma(mate_copies),
        ],
    )
    index = pltpu.SMEM((blocks * most + 2 * UNROLL,), i32)
    ready = [vmem((WIDTH, TILE), f32)] * UNROLL
    pots = shape((blocks, held_blk, WIDTH), f32)
    rp, xt2, cl = call(
        functools.partial(stats_kernel, dims),
        (pots, shape((held, WIDTH, depth), bf16), shape((tiles, TILE), f32)),
        (pairs, all_counts, xt, y, sq),
        [
            vmem((held, WIDTH, LANES), f32), vmem((held, WIDTH, LANES), f32),
            vmem((tiles + 1, 8, TILE), f32), vmem((tiles + 1, 8, TILE), f32), index, index, *ready,
        ],
    )
    level, home = exchange(
        functools.partial(merge_kernel, counts, feat), 1, (shape((tiles + 8, TILE), f32), pots), (rp, cl),
        [vmem((blocks, tiles, TILE), f32), *dma(2 * (blocks - 1))],
    )
    line = shape((1, cells_blk), f32)
    fnum, fden, bnum, bden, row_out, col_out = call(
        functools.partial(plan_kernel, dims),
        (
            shape((blocks, progs, held_blk * WIDTH), bf16), pots,
            shape((blocks, tiles_blk, progs, TILE), bf16), shape((blocks, tiles_blk, TILE), f32), line, line,
        ),
        (pairs, all_counts, xt2, y, level, ext_next, ext_own, column_pot, home),
        [vmem((held, ext, WIDTH), f32), vmem((tiles + 1, ext, TILE), f32), index, index, *ready],
    )
    num, den = vmem((tiles_blk, progs, TILE), bf16), vmem((tiles_blk, TILE), f32)
    smoothed = exchange(
        functools.partial(finish_kernel, counts), 2, shape((progs, cells_blk), bf16), (fnum, fden, bnum, bden),
        [
            vmem((blocks, progs, held_blk * WIDTH), bf16), vmem((blocks, held_blk, WIDTH), f32),
            vmem((2, tiles_blk, progs, TILE), bf16), vmem((2, tiles_blk, TILE), f32),
            vmem((tiles_blk, progs, TILE), f32), den, num, den, num, den, num, den, num, den,
            *dma(6 + 4 * (tiles_blk + 1)),
        ],
    )
    return smoothed[None], row_out, col_out


def solution(mesh):
    in_specs = (
        P("sec", None, "blk"),
        P("sec", None, "blk"),
        P("sec", "blk"),
        P(None, "sec", "blk"),
        P("sec", "blk"),
    )
    out_specs = (P("sec", None, "blk"), P("sec", "blk"), P("sec", "blk"))
    return jax.shard_map(body, mesh=mesh, in_specs=in_specs, out_specs=out_specs, check_vma=False)
```

time: 84.7 us -> 65.8 us (0.78)
  the two profiles are of different devices: /device:TPU:0 before, /device:TPU:8 now
where the time goes in v1:
time: 65.8 us; the launch traced here: 64.9 us
  Pallas kernels  62.1 us (94%)
  local copies, waits for them, and re-layouts  1.57 us (2%)
  between operations  1.3 us (2%)
    pallas_call x3, Pallas kernels, exchange(): pl.pallas_call(kernel, out_shape=out_shape, in_specs=in_vmem(len(operands...  42.5 us
    pallas_call x2, Pallas kernels, call(): pl.pallas_call(kernel, out_shape=out_shape, in_specs=[pl.BlockSpec(memory...  19.5 us
    unnamed x1, local copies, waits for them, and re-layouts  1.57 us

profile of v1, /device:TPU:8, one launch (start us, length us, event | category | flops | bytes accessed | tf_op | source)
XLA Modules:
  0.0 64.9 jit_solution(631390303042600846)
XLA Ops:
  1.3 22.0 %shard_map.76 = (bf16[8,256,64]{2,1,0:T(8,128)(2,1)}, bf16[17,64,512]{2,1,0:T(8,128)(2,1)}, f32[4,2,256]{2,1,0:T(2,128)}, bf16[17,48,512]{2,1,0:T(8,128)(2,1)}, ...) custom-call(bf16[52,2048]{1,0:T(8,128)(2,1)} %bitcast.4, bf16[32,2048]{1,0:T(8,128)(2,1)} %bitcast.5, ...), custom_call_target="tpu_custom_call" | custom-call | tf_op jit(solution)/shard_map/pallas_call | solution.py:541
  23.3 11.0 %shard_map.77 = (f32[4,2,256]{2,1,0:T(2,128)}, bf16[8,256,64]{2,1,0:T(8,128)(2,1)}, f32[16,512]{1,0:T(8,128)}) custom-call(s32[4,2,1,28]{3,2,1,0:T(1,128)} %get-tuple-element.21.pairs_ref, s32[4,1,1]{2,1,0:T(1,128)} %get-tuple-element.22.counts_ref, bf16[8,256,64]{2,1,0:T(8,128)(2,1)} %get-tuple-element.23.xt_ref, ...), custom_call_target="tpu_custom_call" | custom-call | tf_op jit(solution)/shard_map/pallas_call | solution.py:549
  34.2 6.0 %shard_map.78 = (f32[24,512]{1,0:T(8,128)}, f32[4,2,256]{2,1,0:T(2,128)}) custom-call(f32[4,2,256]{2,1,0:T(2,128)} %get-tuple-element.27.rp_ref, f32[16,512]{1,0:T(8,128)} %get-tuple-element.28.cl_ref), custom_call_target="tpu_custom_call" | custom-call | tf_op jit(solution)/shard_map/pallas_call | solution.py:541
  40.3 8.6 %shard_map.79 = (bf16[4,32,512]{2,1,0:T(8,128)(2,1)}, f32[4,2,256]{2,1,0:T(2,128)}, bf16[4,4,32,512]{3,2,1,0:T(8,128)(2,1)}, f32[4,4,512]{2,1,0:T(4,128)}, f32[1,2048]{1,0:T(1,128)}, /*index=5*/f32[1,2048]{1,0:T(1,128)}) custom-call(s32[4,2,1,28]{3,2,1,0:T(1,128)} %get-tuple-element.21.pairs_ref, s32[4,1,1]{2,1,0:T(1,128)} %get-tuple-element.22.counts_ref, ...), custom_call_target="tpu_custom_call" | custom-call | tf_op jit(solution)/shard_map/pallas_call | solution.py:549
  48.8 14.5 %shard_map.80 = bf16[32,2048]{1,0:T(8,128)(2,1)} custom-call(bf16[4,32,512]{2,1,0:T(8,128)(2,1)} %get-tuple-element.33.fnum_ref, f32[4,2,256]{2,1,0:T(2,128)} %get-tuple-element.34.fden_ref, bf16[4,4,32,512]{3,2,1,0:T(8,128)(2,1)} %get-tuple-element.35.bnum_ref, f32[4,4,512]{2,1,0:T(4,128)} %get-tuple-element.36.bden_ref), custom_call_target="tpu_custom_call" | custom-call | tf_op jit(solution)/shard_map/pallas_call | solution.py:541
  63.4 1.6 %copy.10 = bf16[1,32,2048]{2,1,0:T(8,128)(2,1)} copy(bf16[1,32,2048]{2,1,0:T(8,128)(2,1)} %bitcast.3) | data formatting | bytes 262144

commit v2 on v1

--- a/solution.py
+++ b/solution.py
@@ -16,6 +16,7 @@
 SPLITS = 2
 WIDTH = TILE // SPLITS
 LANES = 128
+VMEM_LIMIT = 24 << 20
 MESH = pl.DeviceIdType.MESH
 
 
@@ -93,7 +94,7 @@
 
 def gather_kernel(counts, x_ref, prog_ref, pot_ref, pair_ref, count_ref,
                   xt_ref, y_ref, sq_ref, ext_next_ref, ext_own_ref, pairs_ref, counts_ref,
-                  xs, progs_all, own_x, own_p, pots, build, send_sem, recv_sem, mate_send, mate_recv):
+                  xs, progs_all, own_x, own_p, pots, build, send_sem, recv_sem, mate_send, mate_recv, local_sem):
     n_sec, blocks = counts
     sec, blk = lax.axis_index("sec"), lax.axis_index("blk")
     feat, cells_blk = x_ref.shape
@@ -105,6 +106,14 @@
     held_blk = tiles_blk * SPLITS // blocks
     has_to, has_from = sec > 0, sec < n_sec - 1
     core, across, corner = mates = mates_of(blk, blocks)
+    moves = [(pot_ref, pots.at[blk]), (pair_ref, pairs_ref.at[blk]), (count_ref, counts_ref.at[blk])]
+    for place in range(held_blk):
+        start = pl.multiple_of(lane_of(blk, place, blocks), WIDTH)
+        moves.append((x_ref.at[:, pl.ds(start, WIDTH)], own_x.at[blk, place]))
+        moves.append((prog_ref.at[:, pl.ds(start, WIDTH)], own_p.at[blk, place]))
+    locals_ = [pltpu.make_async_copy(src, dst, local_sem.at[n]) for n, (src, dst) in enumerate(moves)]
+    for copy in locals_:
+        copy.start()
     greet(
         [(has_to, sec - 1, blk), (has_from, sec + 1, blk)] + [(sec >= 0, sec, mate) for mate in mates]
     )
@@ -151,13 +160,8 @@
     row = lax.broadcasted_iota(jnp.int32, (depth, TILE), 0)
     y_ref[tiles] = jnp.where(row == aux, NEG, 0.0).astype(jnp.bfloat16)
     ext_next_ref[tiles] = jnp.zeros(ext_next_ref.shape[1:], jnp.bfloat16)
-    for place in range(held_blk):
-        start = pl.multiple_of(lane_of(blk, place, blocks), WIDTH)
-        own_x[blk, place] = x_ref[:, pl.ds(start, WIDTH)]
-        own_p[blk, place] = prog_ref[:, pl.ds(start, WIDTH)]
-    pots[blk] = pot_ref[...]
-    pairs_ref[blk] = pair_ref[...]
-    counts_ref[blk] = count_ref[...]
+    for copy in locals_:
+        copy.wait()
 
     def build_own(owner):
         for place in range(held_blk):
@@ -400,11 +404,11 @@
     over_pairs(groups, ready, xt_ref, y_ref, mine, other, use)
     for row in range(held):
         owner, place = row // held_blk, row % held_blk
-        fnum_ref[owner, :, place * WIDTH : (place + 1) * WIDTH] = acc_row[row, 0:progs, :].astype(jnp.bfloat16)
+        fnum_ref[owner, :, place * WIDTH : (place + 1) * WIDTH] = acc_row[row, 0:progs, :]
         fden_ref[owner, place : place + 1, :] = acc_row[row, progs : progs + 1, :]
     for col in range(tiles):
         owner, place = col // tiles_blk, col % tiles_blk
-        bnum_ref[owner, place] = acc_col[col, 0:progs, :].astype(jnp.bfloat16)
+        bnum_ref[owner, place] = acc_col[col, 0:progs, :]
         bden_ref[owner, place : place + 1, :] = acc_col[col, progs : progs + 1, :]
 
 
@@ -462,28 +466,32 @@
         for t in order:
             pair(t, False).start()
 
-    for k in (1, 2, 0):
-        for n in range(2):
-            homeward(k, n).start()
     hn[blk] = fnum_ref[blk]
     hd[blk] = fden_ref[blk]
+    far, near = 2 * (1 - side) + me, 2 * side + me
 
     @pl.when(has_to)
     def _():
-        far, near = 2 * (1 - side) + me, 2 * side + me
         for t in order:
             pair(t, True).wait_recv()
             if t == tiles_blk:
                 go_den[...] = bden_ref[far] + ad[0]
             else:
-                go[t] = (bnum_ref[far, t].astype(jnp.float32) + an[0, t].astype(jnp.float32)).astype(jnp.bfloat16)
+                go[t] = (bnum_ref[far, t] + an[0, t]).astype(jnp.bfloat16)
             cross(t).start()
+
+    for k in (1, 2, 0):
+        for n in range(2):
+            homeward(k, n).start()
+
+    @pl.when(has_to)
+    def _():
         for t in order:
             pair(t, False).wait_recv()
             if t == tiles_blk:
                 keep_den[...] = bden_ref[near] + ad[1]
             else:
-                keep[t] = bnum_ref[near, t].astype(jnp.float32) + an[1, t].astype(jnp.float32)
+                keep[t] = bnum_ref[near, t] + an[1, t]
         for t in order:
             cross(t).wait_recv()
             if t == tiles_blk:
@@ -514,7 +522,7 @@
         here = slice(place * WIDTH, (place + 1) * WIDTH)
         for n, owner in enumerate(owners):
             part = slice(n * WIDTH, (n + 1) * WIDTH)
-            number = hn[owner, :, here].astype(jnp.float32) + cn[t, :, part].astype(jnp.float32)
+            number = hn[owner, :, here] + cn[t, :, part].astype(jnp.float32)
             weight = hd[owner, place : place + 1, :] + cd[t : t + 1, part]
             start = t * TILE + n * WIDTH
             out_ref[:, start : start + WIDTH] = (number / weight).astype(jnp.bfloat16)
@@ -532,15 +540,14 @@
             onward(t).wait_send()
 
 
-def in_vmem(count):
-    return [pl.BlockSpec(memory_space=pltpu.VMEM)] * count
-
-
-def exchange(kernel, number, out_shape, operands, scratch):
+def exchange(kernel, number, out_shape, operands, scratch, space=pltpu.VMEM):
     outs = jax.tree.map(lambda _: pl.BlockSpec(memory_space=pltpu.VMEM), out_shape)
     return pl.pallas_call(
-        kernel, out_shape=out_shape, in_specs=in_vmem(len(operands)), out_specs=outs, scratch_shapes=scratch,
-        compiler_params=pltpu.CompilerParams(collective_id=number, has_side_effects=True),
+        kernel, out_shape=out_shape, in_specs=[pl.BlockSpec(memory_space=space)] * len(operands),
+        out_specs=outs, scratch_shapes=scratch,
+        compiler_params=pltpu.CompilerParams(
+            collective_id=number, has_side_effects=True, vmem_limit_bytes=VMEM_LIMIT
+        ),
     )(*operands)
 
 
@@ -548,8 +555,10 @@
     outs = jax.tree.map(lambda _: pl.BlockSpec(memory_space=pltpu.VMEM), out_shape)
     return pl.pallas_call(
         kernel, out_shape=out_shape,
-        in_specs=[pl.BlockSpec(memory_space=pltpu.SMEM)] * 2 + in_vmem(len(operands) - 2),
+        in_specs=[pl.BlockSpec(memory_space=pltpu.SMEM)] * 2
+        + [pl.BlockSpec(memory_space=pltpu.VMEM)] * (len(operands) - 2),
         out_specs=outs, scratch_shapes=scratch,
+        compiler_params=pltpu.CompilerParams(vmem_limit_bytes=VMEM_LIMIT),
     )(*operands)
 
 
@@ -583,7 +592,7 @@
             shape((blocks, 2, 1, most), i32),
             shape((blocks, 1, 1), i32),
         ),
-        (features[0], programs[0], column_pot, tile_pairs, pair_counts),
+        [pltpu.with_memory_space_constraint(part, pltpu.HBM) for part in (features[0], programs[0], column_pot, tile_pairs)] + [pair_counts],
         [
             vmem((blocks, feat, cells_blk), bf16),
             vmem((blocks, progs, cells_blk), bf16),
@@ -591,8 +600,9 @@
             vmem((blocks, held_blk, progs, WIDTH), bf16),
             vmem((blocks, 1, cells_blk), bf16),
             vmem((depth, WIDTH), f32),
-            *dma(4 * (FEAT_CHUNKS + PROG_CHUNKS)), *dma(mate_copies),
+            *dma(4 * (FEAT_CHUNKS + PROG_CHUNKS)), *dma(mate_copies), pltpu.SemaphoreType.DMA((2 * held_blk + 3,)),
         ],
+        pltpu.HBM,
     )
     index = pltpu.SMEM((blocks * most + 2 * UNROLL,), i32)
     ready = [vmem((WIDTH, TILE), f32)] * UNROLL
@@ -614,8 +624,8 @@
     fnum, fden, bnum, bden, row_out, col_out = call(
         functools.partial(plan_kernel, dims),
         (
-            shape((blocks, progs, held_blk * WIDTH), bf16), pots,
-            shape((blocks, tiles_blk, progs, TILE), bf16), shape((blocks, tiles_blk, TILE), f32), line, line,
+            shape((blocks, progs, held_blk * WIDTH), f32), pots,
+            shape((blocks, tiles_blk, progs, TILE), f32), shape((blocks, tiles_blk, TILE), f32), line, line,
         ),
         (pairs, all_counts, xt2, y, level, ext_next, ext_own, column_pot, home),
         [vmem((held, ext, WIDTH), f32), vmem((tiles + 1, ext, TILE), f32), index, index, *ready],
@@ -624,8 +634,8 @@
     smoothed = exchange(
         functools.partial(finish_kernel, counts), 2, shape((progs, cells_blk), bf16), (fnum, fden, bnum, bden),
         [
-            vmem((blocks, progs, held_blk * WIDTH), bf16), vmem((blocks, held_blk, WIDTH), f32),
-            vmem((2, tiles_blk, progs, TILE), bf16), vmem((2, tiles_blk, TILE), f32),
+            vmem((blocks, progs, held_blk * WIDTH), f32), vmem((blocks, held_blk, WIDTH), f32),
+            vmem((2, tiles_blk, progs, TILE), f32), vmem((2, tiles_blk, TILE), f32),
             vmem((tiles_blk, progs, TILE), f32), den, num, den, num, den, num, den, num, den,
             *dma(6 + 4 * (tiles_blk + 1)),
         ],

time: 65.8 us -> 55.8 us (0.85)
  the two profiles are of different devices: /device:TPU:8 before, /device:TPU:0 now
where the time goes in v2:
time: 55.8 us; the launch traced here: 55.6 us
  Pallas kernels  53.6 us (96%)
  between operations  1.34 us (2%)
  local copies, waits for them, and re-layouts  0.66 us (1%)
    pallas_call x3, Pallas kernels, exchange(): pl.pallas_call(kernel, out_shape=out_shape, in_specs=[pl.BlockSpec(memory...  37 us
    pallas_call x2, Pallas kernels, call(): pl.pallas_call(kernel, out_shape=out_shape, in_specs=[pl.BlockSpec(memory...  16.6 us

profile of v2, /device:TPU:0, one launch (start us, length us, event | category | flops | bytes accessed | tf_op | source)
XLA Modules:
  0.0 55.6 jit_solution(3066114609877747152)
XLA Ops:
  0.6 0.0 copy-start
  1.3 21.3 %shard_map.76 = (bf16[8,256,64]{2,1,0:T(8,128)(2,1)S(1)}, bf16[17,64,512]{2,1,0:T(8,128)(2,1)S(1)}, f32[4,2,256]{2,1,0:T(2,128)S(1)}, bf16[17,48,512]{2,1,0:T(8,...) custom-call(bf16[52,2048]{1,0:T(8,128)(2,1)} %bitcast.4, ...), custom_call_target="tpu_custom_call" | custom-call | tf_op jit(solution)/shard_map/pallas_call | solution.py:545
  22.6 9.6 %shard_map.77 = (f32[4,2,256]{2,1,0:T(2,128)S(1)}, bf16[8,256,64]{2,1,0:T(8,128)(2,1)S(1)}, f32[16,512]{1,0:T(8,128)S(1)}) custom-call(s32[4,2,1,28]{3,2,1,0:T(1,128)S(1)} %get-tuple-element.21.pairs_ref, s32[4,1,1]{2,1,0:T(1,128)S(1)} %get-tuple-element.22.counts_ref, bf16[8,256,64]{2,1,0:T(8,128)(2,1)S(1)} %get-tuple-element.23.xt_ref, ...), custom_call_target="tpu_custom_call" | custom-call | tf_op jit(solution)/shard_map/pallas_call | solution.py:556
  32.2 4.7 %shard_map.78 = (f32[24,512]{1,0:T(8,128)S(1)}, f32[4,2,256]{2,1,0:T(2,128)S(1)}) custom-call(f32[4,2,256]{2,1,0:T(2,128)S(1)} %get-tuple-element.27.rp_ref, f32[16,512]{1,0:T(8,128)S(1)} %get-tuple-element.28.cl_ref), custom_call_target="tpu_custom_call" | custom-call | tf_op jit(solution)/shard_map/pallas_call | solution.py:545
  36.8 0.0 copy-done
  36.8 7.0 %shard_map.79 = (f32[4,32,512]{2,1,0:T(8,128)S(1)}, f32[4,2,256]{2,1,0:T(2,128)S(1)}, f32[4,4,32,512]{3,2,1,0:T(8,128)S(1)}, f32[4,4,512]{2,1,0:T(4,128)S(1)}, f32[1,2048]{1,0:T(1,128)}, /*index=5*/f32[1,2048]{1,0:T(1,128)}) custom-call(s32[4,2,1,28]{3,2,1,0:T(1,128)S(1)} %get-tuple-element.21.pairs_ref, s32[4,1,1]{2,1,0:T(1,128)S(1)} %get-tuple-element.22.counts_ref, ...), custom_call_target="tpu_custom_call" | custom-call | tf_op jit(solution)/shard_map/pallas_call | solution.py:556
  43.9 11.0 %shard_map.80 = bf16[32,2048]{1,0:T(8,128)(2,1)S(1)} custom-call(f32[4,32,512]{2,1,0:T(8,128)S(1)} %get-tuple-element.33.fnum_ref, f32[4,2,256]{2,1,0:T(2,128)S(1)} %get-tuple-element.34.fden_ref, f32[4,4,32,512]{3,2,1,0:T(8,128)S(1)} %get-tuple-element.35.bnum_ref, f32[4,4,512]{2,1,0:T(4,128)S(1)} %get-tuple-element.36.bden_ref), custom_call_target="tpu_custom_call" | custom-call | tf_op jit(solution)/shard_map/pallas_call | solution.py:545
  54.9 0.7 %copy.10 = bf16[1,32,2048]{2,1,0:T(8,128)(2,1)} copy(bf16[1,32,2048]{2,1,0:T(8,128)(2,1)S(1)} %bitcast.3) | data formatting | bytes 262144
Async XLA Ops:
  0.6 36.2 %copy-start = (bf16[1,2048]{1,0:T(2,128)(2,1)S(1)}, bf16[1,2048]{1,0:T(2,128)(2,1)}, u32[]{:S(2)}) copy-start(bf16[1,2048]{1,0:T(2,128)(2,1)} %pot_ref.3) | copy-start | bytes 12292

commit v3 on v2

v3 whole, which is shorter than its diff:
```python
import functools
import math

import jax
import jax.numpy as jnp
from jax import lax
from jax.experimental import pallas as pl
from jax.experimental.pallas import tpu as pltpu
from jax.sharding import PartitionSpec as P

TILE = 512
EPSILON = 0.05
LOG2E = math.log2(math.e)
NEG = -1e30
UNROLL = 4
SPLITS = 2
WIDTH = TILE // SPLITS
LANES = 128
VMEM_LIMIT = 24 << 20
MESH = pl.DeviceIdType.MESH


def depth_of(feat):
    return -(-(feat + 8) // 16) * 16


def ext_of(progs):
    return -(-(progs + 1) // 16) * 16


def gain_of(feat):
    return 2.0 * LOG2E / (feat * EPSILON)


def split3(value):
    hi = value.astype(jnp.bfloat16).astype(jnp.float32)
    rest = value - hi
    mid = rest.astype(jnp.bfloat16).astype(jnp.float32)
    return hi, mid, rest - mid


def lists_width(blocks, most):
    return -(-(blocks * most + 3 * UNROLL) // LANES) * LANES


def rows_of(pieces, width):
    index = lax.broadcasted_iota(jnp.int32, (8, width), 0)
    block = jnp.zeros((8, width), jnp.float32)
    for place, piece in enumerate(pieces):
        block = jnp.where(index == place, piece, block)
    return block


def sum_squares(cells):
    return jnp.sum(cells * cells, axis=0, keepdims=True)


def lane_of(owner, place, blocks):
    kinds = blocks // SPLITS
    return (place * kinds + owner // SPLITS) * TILE + (owner % SPLITS) * WIDTH


def greet(targets):
    barrier = pltpu.get_barrier_semaphore()
    expected = jnp.int32(0)
    for used, sec, blk in targets:

        @pl.when(used)
        def _():
            pl.semaphore_signal(barrier, inc=1, device_id=(sec, blk), device_id_type=MESH)

        expected = expected + jnp.where(used, 1, 0)
    pl.semaphore_wait(barrier, expected)


def send(src, dst, sems, place, sec, blk):
    return pltpu.make_async_remote_copy(
        src_ref=src, dst_ref=dst, send_sem=sems[0].at[place], recv_sem=sems[1].at[place],
        device_id=(sec, blk), device_id_type=MESH,
    )


def mates_of(blk, blocks):
    core = blk + 1 - 2 * (blk % 2)
    across = (blk + 2) % blocks
    corner = core + 2 - 4 * (core // 2)
    return core, across, corner


def ext_tail(progs, width):
    index = lax.broadcasted_iota(jnp.int32, (ext_of(progs) - progs, width), 0)
    return jnp.where(index == 0, 1.0, 0.0).astype(jnp.bfloat16)


FEAT_CHUNKS = 4
PARTS = 1


def compact_lists(pairs_ref, counts_ref, lists_ref, kind, blocks, tiles_blk):
    most = pairs_ref.shape[3]
    width = lists_ref.shape[1]
    kinds = blocks // SPLITS
    tiles = blocks * tiles_blk
    f32, bf16 = jnp.float32, jnp.bfloat16
    slot = lax.broadcasted_iota(jnp.int32, (1, most), 1)
    before = lax.broadcasted_iota(jnp.int32, (most, most), 0) < lax.broadcasted_iota(jnp.int32, (most, most), 1)
    before = jnp.where(before, 1.0, 0.0).astype(bf16)
    spot = lax.broadcasted_iota(jnp.int32, (width, most), 0).astype(f32)
    line = lax.broadcasted_iota(jnp.int32, (8, most), 0)
    start = jnp.full((1, 1), UNROLL, f32)
    found = jnp.zeros((8, width), f32)
    for block in range(blocks):
        row = pairs_ref[block, 0] + block * tiles_blk
        keep = jnp.logical_and(slot < counts_ref[block], row % kinds == kind)
        flag = jnp.where(keep, 1.0, 0.0)
        flags = jnp.broadcast_to(flag, (8, most))
        rank = jnp.dot(flags.astype(bf16), before, preferred_element_type=f32)[0:1] + start
        hits = jnp.where(keep, jnp.where(spot == rank, 1.0, 0.0), 0.0).astype(bf16)
        held, across = (row // kinds).astype(f32), pairs_ref[block, 1].astype(f32)
        values = jnp.where(line == 0, held, jnp.where(line == 1, across, 1.0)).astype(bf16)
        found += lax.dot_general(values, hits, (((1,), (1,)), ((), ())), preferred_element_type=f32)
        start = start + jnp.sum(flag, axis=1, keepdims=True)
    index = lax.broadcasted_iota(jnp.int32, (8, width), 0)
    other = jnp.where(found[2:3] > 0.0, found[1:2], float(tiles))
    table = jnp.where(index == 0, found[0:1], jnp.where(index == 1, other, start - UNROLL))
    lists_ref[...] = table.astype(jnp.int32)


def gather_kernel(counts, x_ref, prog_ref, pot_ref, pair_ref, count_ref,
                  xrec_ref, y_ref, yt_ref, sq_ref, pack_ref, pown_ref, lists_ref,
                  xs, own_x, pots, pairs, pair_counts, xbuild, ybuild,
                  send_sem, recv_sem, mate_send, mate_recv, local_sem):
    n_sec, blocks = counts
    sec, blk = lax.axis_index("sec"), lax.axis_index("blk")
    feat, cells_blk = x_ref.shape
    depth = depth_of(feat)
    aux = depth - 8
    gain = gain_of(feat)
    tiles_blk = cells_blk // TILE
    tiles = tiles_blk * blocks
    held_blk = tiles_blk * SPLITS // blocks
    piece = held_blk * WIDTH
    has_to, has_from = sec > 0, sec < n_sec - 1
    core, across, corner = mates = mates_of(blk, blocks)
    me = blk % 2
    mine_at = pl.multiple_of(me * cells_blk, LANES)
    beside_at = pl.multiple_of(SPLITS * cells_blk + me * piece, LANES)
    own_at = pl.multiple_of(me * piece, LANES)

    def prog_piece(owner, place):
        return prog_ref.at[:, pl.ds(pl.multiple_of(lane_of(owner, place, blocks), WIDTH), WIDTH)]

    moves = [(pot_ref, pots.at[blk]), (pair_ref, pairs.at[blk]), (count_ref, pair_counts.at[blk])]
    for place in range(held_blk):
        start = pl.multiple_of(lane_of(blk, place, blocks), WIDTH)
        moves.append((x_ref.at[:, pl.ds(start, WIDTH)], own_x.at[blk, place]))
    for place in range(held_blk):
        moves.append((prog_piece(blk, place), pown_ref.at[:, pl.ds(own_at + place * WIDTH, WIDTH)]))
        moves.append((prog_piece(across, place), pack_ref.at[:, pl.ds(beside_at + place * WIDTH, WIDTH)]))
    locals_ = [pltpu.make_async_copy(src, dst, local_sem.at[n]) for n, (src, dst) in enumerate(moves)]
    for copy in locals_:
        copy.start()
    greet(
        [(has_to, sec - 1, blk), (has_from, sec + 1, blk)] + [(sec >= 0, sec, mate) for mate in mates]
    )
    sems, mate_sems = (send_sem, recv_sem), (mate_send, mate_recv)
    feat_step = cells_blk // FEAT_CHUNKS
    chunks = [(n * feat_step, feat_step) for n in range(FEAT_CHUNKS)]
    last = 4 * len(chunks)

    def first(c):
        start, size = chunks[c]
        return send(
            x_ref.at[:, start : start + size], xs.at[blk, :, start : start + size], sems, 4 * c, sec - 1, blk
        )

    def first_programs():
        return send(prog_ref, pack_ref.at[:, pl.ds(mine_at, cells_blk)], sems, last, sec - 1, blk)

    def share_programs():
        slot = pack_ref.at[:, pl.ds(mine_at, cells_blk)]
        return send(slot, slot, sems, last + 1, sec, core)

    def share(c, kind):
        start, size = chunks[c]
        slot = xs.at[across if kind == 2 else blk, :, start : start + size]
        return send(slot, slot, sems, 4 * c + 1 + kind, sec, across if kind == 0 else core)

    def to_mate(k):
        mate = mates[k]
        copies = [(pot_ref, pots.at[blk]), (pair_ref, pairs.at[blk]), (count_ref, pair_counts.at[blk])]
        for place in range(held_blk):
            start = pl.multiple_of(lane_of(mate, place, blocks), WIDTH)
            copies.append((x_ref.at[:, pl.ds(start, WIDTH)], own_x.at[blk, place]))
        per = len(copies)
        return [send(src, dst, mate_sems, per * k + n, sec, mate) for n, (src, dst) in enumerate(copies)]

    def pieces_to_core():
        base = 3 * (held_blk + 3)
        copies = []
        for place in range(held_blk):
            copies.append((prog_piece(core, place), pown_ref.at[:, pl.ds(own_at + place * WIDTH, WIDTH)]))
            copies.append((prog_piece(corner, place), pack_ref.at[:, pl.ds(beside_at + place * WIDTH, WIDTH)]))
        return [send(src, dst, mate_sems, base + n, sec, core) for n, (src, dst) in enumerate(copies)]

    @pl.when(has_to)
    def _():
        for c in range(len(chunks)):
            first(c).start()
        first_programs().start()

    to_mates = [to_mate(k) for k in range(3)]
    for n in range(len(to_mates[0])):
        for k in (1, 2, 0):
            to_mates[k][n].start()
    to_core = pieces_to_core()
    for copy in to_core:
        copy.start()

    xbuild[...] = jnp.zeros_like(xbuild)
    xbuild[aux:depth, :] = rows_of([1.0] * 3, WIDTH)
    ybuild[...] = jnp.zeros_like(ybuild)
    row = lax.broadcasted_iota(jnp.int32, y_ref.shape[1:], 0)
    y_ref[tiles] = jnp.where(row == aux, NEG, 0.0).astype(jnp.bfloat16)
    lane = lax.broadcasted_iota(jnp.int32, yt_ref.shape[1:], 1)
    yt_ref[tiles] = jnp.where(lane == aux, NEG, 0.0).astype(jnp.bfloat16)
    for copy in locals_:
        copy.wait()

    def build_own(owner):
        for place in range(held_blk):
            cells = own_x[owner, place].astype(jnp.float32)
            scaled = cells * gain
            high = scaled.astype(jnp.bfloat16).astype(jnp.float32)
            xbuild[0:feat, :] = high
            xbuild[depth : depth + feat, :] = scaled - high
            xrec_ref[owner * held_blk + place] = xbuild[...].astype(jnp.bfloat16)
            sq_ref[owner, place : place + 1, :] = sum_squares(cells)

    ones = jnp.ones((1, TILE), jnp.float32)

    def build_next(owner, c):
        begin, size = chunks[c]
        for start in range(begin, begin + size, TILE):
            tile = owner * tiles_blk + start // TILE
            cells = xs[owner, :, start : start + TILE].astype(jnp.float32)
            pot = pots[owner, :, start : start + TILE].astype(jnp.float32)
            bias = pot * (LOG2E / EPSILON) - sum_squares(cells) * (gain * 0.5)
            ybuild[0:feat, :] = cells
            ybuild[depth : depth + feat, :] = cells
            ybuild[aux:depth, :] = rows_of(split3(bias) + (ones,) * 3, TILE)
            y_ref[tile] = ybuild[...].astype(jnp.bfloat16)
            yt_ref[tile] = ybuild[...].T.astype(jnp.bfloat16)

    for k in range(3):
        for copy in to_mates[k][:3]:
            copy.wait_recv()
    compact_lists(pairs, pair_counts, lists_ref, blk // SPLITS, blocks, tiles_blk)
    build_own(blk)

    @pl.when(has_from)
    def _():
        for turn in range(len(chunks) + 2):
            if turn < len(chunks):
                first(turn).wait_recv()
                share(turn, 0).start()
                share(turn, 1).start()
                build_next(blk, turn)
            if 0 <= turn - 1 < len(chunks):
                share(turn - 1, 0).wait_recv()
                share(turn - 1, 2).start()
                build_next(across, turn - 1)
                share(turn - 1, 1).wait_recv()
                build_next(core, turn - 1)
            if turn == len(chunks):
                first_programs().wait_recv()
                share_programs().start()
            if 0 <= turn - 2 < len(chunks):
                share(turn - 2, 2).wait_recv()
                build_next(corner, turn - 2)
        share_programs().wait_recv()

    @pl.when(jnp.logical_not(has_from))
    def _():
        pack_ref[:, 0 : SPLITS * cells_blk] = jnp.zeros((pack_ref.shape[0], SPLITS * cells_blk), jnp.bfloat16)

    for k, mate in enumerate(mates):
        for copy in to_mates[k][3:]:
            copy.wait_recv()
        build_own(mate)
    for copy in to_core:
        copy.wait_recv()

    @pl.when(has_to)
    def _():
        for c in range(len(chunks)):
            first(c).wait_send()
        first_programs().wait_send()

    @pl.when(has_from)
    def _():
        for c in range(len(chunks)):
            for kind in range(3):
                share(c, kind).wait_send()
        share_programs().wait_send()

    for k in range(3):
        for copy in to_mates[k]:
            copy.wait_send()
    for copy in to_core:
        copy.wait_send()


def rounds_of(lists_ref):
    return (lists_ref[2, 0] + UNROLL - 1) // UNROLL


def stats_kernel(dims, lists_ref, xrec_ref, y_ref, yt_ref, sq_ref, rp_ref, xt_out, cl_ref,
                 top_row, sum_row, top_col, sum_col, tops_row, tops_col, *ready):
    feat, blocks, tiles_blk = dims
    tiles = blocks * tiles_blk
    held_blk = tiles_blk * SPLITS // blocks
    held = blocks * held_blk
    half_gain = gain_of(feat) * 0.5
    depth = depth_of(feat)
    aux = depth - 8
    at_end = lax.axis_index("sec") == lax.axis_size("sec") - 1
    rounds = rounds_of(lists_ref)
    for ref in (top_row, top_col):
        ref[...] = jnp.full_like(ref, NEG)
    for ref in (sum_row, sum_col):
        ref[...] = jnp.zeros_like(ref)

    def sweep(scores_of, ready, tops, top_acc, sum_acc, by_row):
        rows, width = ready[0].shape
        size = rows // PARTS

        def make(at, slot):
            best = None
            for start in range(0, rows, size):
                here = pl.ds(start, size)
                scores = scores_of(lists_ref[0, at], lists_ref[1, at], here)
                ready[slot][here, :] = scores
                found = jnp.max(scores.reshape(size // 8, 8, width), axis=0)
                best = found if best is None else jnp.maximum(best, found)
            tops[slot] = best

        def use(at, slot):
            target = lists_ref[0 if by_row else 1, at]
            old = top_acc[target]
            new = jnp.maximum(old, tops[slot])
            total = sum_acc[target] * jnp.exp2(old - new)
            for start in range(0, rows, size):
                scores = ready[slot][start : start + size, :].reshape(size // 8, 8, width)
                total = total + jnp.sum(jnp.exp2(scores - new[None]), axis=0)
            sum_acc[target] = total
            top_acc[target] = new

        for n in range(UNROLL):
            make(UNROLL + n, n)

        def step(index, carry):
            for n in range(UNROLL):
                at = index * UNROLL + UNROLL + n
                use(at, n)
                make(at + UNROLL, n)
            return carry

        lax.fori_loop(0, rounds, step, 0)

    def level_of(tops, sums):
        top = jnp.max(tops, axis=0, keepdims=True)
        total = jnp.sum(sums * jnp.exp2(tops - top), axis=0, keepdims=True)
        return top, total

    sweep(
        lambda row, col, here: jnp.dot(yt_ref[col, here, :], xrec_ref[row], preferred_element_type=jnp.float32),
        ready[:UNROLL], tops_row, top_row, sum_row, True,
    )
    record_row = lax.broadcasted_iota(jnp.int32, (8, WIDTH), 0)
    for row in range(held):
        owner, place = row // held_blk, row % held_blk
        top, total = level_of(top_row[row], sum_row[row])
        level = top + jnp.log2(total)
        potential = (sq_ref[owner, place : place + 1, :] * half_gain - level) * (EPSILON / LOG2E)
        rp_ref[owner, place : place + 1, :] = jnp.where(at_end, 0.0, potential)
        extra = rows_of((1.0,) * 3 + split3(-level), WIDTH)
        record = xrec_ref[row].astype(jnp.float32)
        record = jnp.concatenate([record[0:aux], extra, record[depth:]], axis=0)
        xt_out[row] = record.T.astype(jnp.bfloat16)
    sweep(
        lambda row, col, here: jnp.dot(xt_out[row, here, :], y_ref[col], preferred_element_type=jnp.float32),
        ready[UNROLL:], tops_col, top_col, sum_col, False,
    )
    for col in range(tiles):
        top, total = level_of(top_col[col], sum_col[col])
        cl_ref[col : col + 1, :] = jnp.where(total > 0.0, top + jnp.log2(total), NEG)


def merge_kernel(counts, rp_ref, cl_ref, level_ref, home_ref, parts, send_sem, recv_sem):
    n_sec, blocks = counts
    sec, blk = lax.axis_index("sec"), lax.axis_index("blk")
    tiles = cl_ref.shape[0]
    mates = mates_of(blk, blocks)
    sems = (send_sem, recv_sem)
    greet([(sec >= 0, sec, mate) for mate in mates])
    copies = []
    for k, mate in enumerate(mates):
        copies.append(send(cl_ref, parts.at[blk], sems, 2 * k, sec, mate))
        copies.append(send(rp_ref.at[mate], home_ref.at[blk], sems, 2 * k + 1, sec, mate))
    for k in (1, 2, 0):
        for copy in copies[2 * k : 2 * k + 2]:
            copy.start()
    parts[blk] = cl_ref[...]
    home_ref[blk] = rp_ref[blk]
    level_ref[tiles:, :] = jnp.zeros((level_ref.shape[0] - tiles, TILE), jnp.float32)
    for copy in copies:
        copy.wait_recv()
    levels = [parts[n] for n in range(blocks)]
    top = functools.reduce(jnp.maximum, levels)
    total = functools.reduce(jnp.add, [jnp.exp2(level - top) for level in levels])
    level_ref[0:tiles, :] = top + jnp.log2(total)
    for copy in copies:
        copy.wait_send()


def plan_kernel(dims, lists_ref, xt_ref, y_ref, level_ref, near_ref, pown_ref, far_ref, pot_ref, home_ref,
                fnum_ref, fden_ref, bnum_ref, bden_ref, rows_ref, cols_ref,
                acc_row, acc_col, ext_next_ref, ext_own_ref, *ready):
    feat, blocks, tiles_blk = dims
    tiles = blocks * tiles_blk
    held_blk = tiles_blk * SPLITS // blocks
    held = blocks * held_blk
    cells_blk = tiles_blk * TILE
    piece = held_blk * WIDTH
    progs = fnum_ref.shape[1]
    kept = acc_row.shape[1]
    at_end = lax.axis_index("sec") == lax.axis_size("sec") - 1
    blk = lax.axis_index("blk")
    side = blk // SPLITS
    rounds = rounds_of(lists_ref)
    scores, plans = ready[:UNROLL], ready[UNROLL:]

    def make(at, place):
        scores[place][...] = jnp.dot(
            xt_ref[lists_ref[0, at]], y_ref[lists_ref[1, at]], preferred_element_type=jnp.float32
        )

    for n in range(UNROLL):
        make(UNROLL + n, n)
        plans[n][...] = jnp.zeros_like(plans[n])
    acc_row[...] = jnp.zeros_like(acc_row)
    acc_col[...] = jnp.zeros_like(acc_col)
    ext_next_ref[tiles] = jnp.zeros(ext_next_ref.shape[1:], jnp.bfloat16)
    for group, nums, owns, shift in ((side, near_ref, pown_ref, 0), (1 - side, far_ref, far_ref, SPLITS * cells_blk)):
        for n in range(SPLITS):
            owner = group * SPLITS + n
            for tile in range(tiles_blk):
                start = n * cells_blk + tile * TILE
                ext_next_ref[owner * tiles_blk + tile, 0:progs, :] = nums[:, start : start + TILE]
                ext_next_ref[owner * tiles_blk + tile, progs:, :] = ext_tail(progs, TILE)
            for place in range(held_blk):
                start = shift + n * piece + place * WIDTH
                ext_own_ref[owner * held_blk + place, 0:progs, :] = owns[:, start : start + WIDTH]
                ext_own_ref[owner * held_blk + place, progs:, :] = ext_tail(progs, WIDTH)
    for owner in range(blocks):
        for place in range(held_blk):
            start = lane_of(owner, place, blocks)
            rows_ref[:, start : start + WIDTH] = home_ref[owner, place : place + 1, :]
    for tile in range(tiles_blk):
        here = slice(tile * TILE, (tile + 1) * TILE)
        level = level_ref[pl.ds(blk * tiles_blk + tile, 1), :]
        potential = pot_ref[:, here].astype(jnp.float32) - level * (EPSILON / LOG2E)
        cols_ref[:, here] = jnp.where(at_end, 0.0, potential)

    def weigh(at, place):
        level = level_ref[pl.ds(lists_ref[1, at], 1), :]
        plans[place][...] = jnp.exp2(scores[place][...] - level).astype(jnp.bfloat16)

    def gather(at, place):
        row, col = lists_ref[0, at], lists_ref[1, at]
        plan = plans[place][...]
        acc_row[row] += lax.dot_general(
            ext_next_ref[col], plan, (((1,), (1,)), ((), ())), preferred_element_type=jnp.float32
        )[0:kept]
        acc_col[col] += jnp.dot(ext_own_ref[row], plan, preferred_element_type=jnp.float32)[0:kept]

    def step(index, carry):
        for n in range(UNROLL):
            at = index * UNROLL + UNROLL + n
            gather(at - UNROLL, n)
            weigh(at, n)
            make(at + UNROLL, n)
        return carry

    lax.fori_loop(0, rounds, step, 0)
    for n in range(UNROLL):
        gather(rounds * UNROLL + n, n)
    for row in range(held):
        owner, place = row // held_blk, row % held_blk
        fnum_ref[owner, :, place * WIDTH : (place + 1) * WIDTH] = acc_row[row, 0:progs, :]
        fden_ref[owner, place : place + 1, :] = acc_row[row, progs : progs + 1, :]
    for col in range(tiles):
        owner, place = col // tiles_blk, col % tiles_blk
        bnum_ref[owner, place] = acc_col[col, 0:progs, :]
        bden_ref[owner, place : place + 1, :] = acc_col[col, progs : progs + 1, :]


def finish_kernel(counts, fnum_ref, fden_ref, bnum_ref, bden_ref, out_ref,
                  hn, hd, an, ad, keep, keep_den, go, go_den, bn, bd, ship, ship_den, cn, cd,
                  send_sem, recv_sem):
    n_sec, blocks = counts
    sec, blk = lax.axis_index("sec"), lax.axis_index("blk")
    tiles_blk = bnum_ref.shape[1]
    held_blk = fden_ref.shape[1]
    kinds = blocks // SPLITS
    has_to, has_from = sec < n_sec - 1, sec > 0
    core, across, corner = mates = mates_of(blk, blocks)
    me, side = blk % 2, blk // 2
    sems = (send_sem, recv_sem)
    greet(
        [(has_to, sec + 1, blk), (has_from, sec - 1, blk)] + [(sec >= 0, sec, mate) for mate in mates]
    )

    def homeward(k, n):
        mate = mates[k]
        src, dst = ((fnum_ref, hn), (fden_ref, hd))[n]
        return send(src.at[mate], dst.at[blk], sems, 2 * k + n, sec, mate)

    steps = tiles_blk + 1
    base = 6

    def pair(t, far):
        place = 1 - side if far else side
        source = 2 * place + 1 - me
        number = base + 2 * t + (0 if far else 1)
        slot = 0 if far else 1
        if t == tiles_blk:
            return send(bden_ref.at[source], ad.at[slot], sems, number, sec, core)
        return send(bnum_ref.at[source, t], an.at[slot, t], sems, number, sec, core)

    def cross(t):
        number = base + 2 * steps + t
        if t == tiles_blk:
            return send(go_den, bd, sems, number, sec, across)
        return send(go.at[t], bn.at[t], sems, number, sec, across)

    def onward(t):
        number = base + 3 * steps + t
        if t == tiles_blk:
            return send(ship_den, cd, sems, number, sec + 1, blk)
        return send(ship.at[t], cn.at[t], sems, number, sec + 1, blk)

    order = [tiles_blk] + list(range(tiles_blk))

    @pl.when(has_to)
    def _():
        for t in order:
            pair(t, True).start()
        for t in order:
            pair(t, False).start()

    hn[blk] = fnum_ref[blk]
    hd[blk] = fden_ref[blk]
    far, near = 2 * (1 - side) + me, 2 * side + me

    @pl.when(has_to)
    def _():
        for t in order:
            pair(t, True).wait_recv()
            if t == tiles_blk:
                go_den[...] = bden_ref[far] + ad[0]
            else:
                go[t] = (bnum_ref[far, t] + an[0, t]).astype(jnp.bfloat16)
            cross(t).start()

    for k in (1, 2, 0):
        for n in range(2):
            homeward(k, n).start()

    @pl.when(has_to)
    def _():
        for t in order:
            pair(t, False).wait_recv()
            if t == tiles_blk:
                keep_den[...] = bden_ref[near] + ad[1]
            else:
                keep[t] = bnum_ref[near, t] + an[1, t]
        for t in order:
            cross(t).wait_recv()
            if t == tiles_blk:
                ship_den[...] = keep_den[...] + bd[...]
            else:
                ship[t] = (keep[t] + bn[t].astype(jnp.float32)).astype(jnp.bfloat16)
            onward(t).start()

    for k in range(3):
        for n in range(2):
            homeward(k, n).wait_recv()

    @pl.when(jnp.logical_not(has_from))
    def _():
        cn[...] = jnp.zeros_like(cn)
        cd[...] = jnp.zeros_like(cd)

    for t in order:

        @pl.when(has_from)
        def _():
            onward(t).wait_recv()

        if t == tiles_blk:
            continue
        place, kind = t // kinds, t % kinds
        owners = [kind * SPLITS + n for n in range(SPLITS)]
        here = slice(place * WIDTH, (place + 1) * WIDTH)
        for n, owner in enumerate(owners):
            part = slice(n * WIDTH, (n + 1) * WIDTH)
            number = hn[owner, :, here] + cn[t, :, part].astype(jnp.float32)
            weight = hd[owner, place : place + 1, :] + cd[t : t + 1, part]
            start = t * TILE + n * WIDTH
            out_ref[:, start : start + WIDTH] = (number / weight).astype(jnp.bfloat16)

    for k in range(3):
        for n in range(2):
            homeward(k, n).wait_send()

    @pl.when(has_to)
    def _():
        for t in range(steps):
            pair(t, True).wait_send()
            pair(t, False).wait_send()
            cross(t).wait_send()
            onward(t).wait_send()


def exchange(kernel, number, out_shape, operands, scratch, space=pltpu.VMEM):
    outs = jax.tree.map(lambda _: pl.BlockSpec(memory_space=pltpu.VMEM), out_shape)
    return pl.pallas_call(
        kernel, out_shape=out_shape, in_specs=[pl.BlockSpec(memory_space=space)] * len(operands),
        out_specs=outs, scratch_shapes=scratch,
        compiler_params=pltpu.CompilerParams(
            collective_id=number, has_side_effects=True, vmem_limit_bytes=VMEM_LIMIT
        ),
    )(*operands)


def call(kernel, out_shape, operands, scratch):
    outs = jax.tree.map(lambda _: pl.BlockSpec(memory_space=pltpu.VMEM), out_shape)
    return pl.pallas_call(
        kernel, out_shape=out_shape,
        in_specs=[pl.BlockSpec(memory_space=pltpu.SMEM)]
        + [pl.BlockSpec(memory_space=pltpu.VMEM)] * (len(operands) - 1),
        out_specs=outs, scratch_shapes=scratch,
        compiler_params=pltpu.CompilerParams(vmem_limit_bytes=VMEM_LIMIT),
    )(*operands)


def body(features, programs, column_pot, tile_pairs, pair_counts):
    feat, cells_blk = features.shape[1:]
    progs = programs.shape[1]
    tiles_blk = cells_blk // TILE
    most = tile_pairs.shape[2]
    blocks, n_sec = lax.axis_size("blk"), lax.axis_size("sec")
    tiles = tiles_blk * blocks
    held_blk = tiles_blk * SPLITS // blocks
    held = blocks * held_blk
    dims = (feat, blocks, tiles_blk)
    counts = (n_sec, blocks)
    depth, ext = depth_of(feat), ext_of(progs)
    f32, bf16, i32 = jnp.float32, jnp.bfloat16, jnp.int32
    shape, vmem = jax.ShapeDtypeStruct, pltpu.VMEM

    def dma(number):
        return [pltpu.SemaphoreType.DMA((number,))] * 2

    piece = held_blk * WIDTH
    kept = -(-(progs + 1) // 8) * 8
    mate_copies = (blocks - 1) * (held_blk + 3) + 2 * held_blk
    packed = SPLITS * (cells_blk + piece)
    spaced = [
        pltpu.with_memory_space_constraint(part, pltpu.HBM)
        for part in (features[0], programs[0], column_pot, tile_pairs)
    ]
    xrec, y, yt, sq, pack, pown, lists = exchange(
        functools.partial(gather_kernel, counts), 0,
        (
            shape((held, 2 * depth, WIDTH), bf16),
            shape((tiles + 1, 2 * depth, TILE), bf16),
            shape((tiles + 1, TILE, 2 * depth), bf16),
            shape((blocks, held_blk, WIDTH), f32),
            shape((progs, packed), bf16),
            shape((progs, SPLITS * piece), bf16),
            shape((8, lists_width(blocks, most)), i32),
        ),
        (*spaced, pair_counts),
        [
            vmem((blocks, feat, cells_blk), bf16),
            vmem((blocks, held_blk, feat, WIDTH), bf16),
            vmem((blocks, 1, cells_blk), bf16),
            vmem((blocks, 2, 1, most), i32),
            vmem((blocks, 1, 1), i32),
            vmem((2 * depth, WIDTH), f32),
            vmem((2 * depth, TILE), f32),
            *dma(4 * FEAT_CHUNKS + 2), *dma(mate_copies), pltpu.SemaphoreType.DMA((3 + 3 * held_blk,)),
        ],
        pltpu.HBM,
    )
    far = lax.ppermute(pack, "blk", [(source, (source + 2) % blocks) for source in range(blocks)])
    pots = shape((blocks, held_blk, WIDTH), f32)
    tall, wide = vmem((TILE, WIDTH), f32), vmem((WIDTH, TILE), f32)
    rp, xt, cl = call(
        functools.partial(stats_kernel, dims),
        (pots, shape((held, WIDTH, 2 * depth), bf16), shape((tiles, TILE), f32)),
        (lists, xrec, y, yt, sq),
        [
            vmem((held, 8, WIDTH), f32), vmem((held, 8, WIDTH), f32),
            vmem((tiles + 1, 8, TILE), f32), vmem((tiles + 1, 8, TILE), f32),
            vmem((UNROLL, 8, WIDTH), f32), vmem((UNROLL, 8, TILE), f32), *[tall] * UNROLL, *[wide] * UNROLL,
        ],
    )
    level, home = exchange(
        functools.partial(merge_kernel, counts), 1, (shape((tiles + 8, TILE), f32), pots), (rp, cl),
        [vmem((blocks, tiles, TILE), f32), *dma(2 * (blocks - 1))],
    )
    line = shape((1, cells_blk), f32)
    flat = vmem((WIDTH, TILE), bf16)
    fnum, fden, bnum, bden, row_out, col_out = call(
        functools.partial(plan_kernel, dims),
        (
            shape((blocks, progs, held_blk * WIDTH), f32), pots,
            shape((blocks, tiles_blk, progs, TILE), f32), shape((blocks, tiles_blk, TILE), f32), line, line,
        ),
        (lists, xt, y, level, pack, pown, far, column_pot, home),
        [
            vmem((held, kept, WIDTH), f32), vmem((tiles + 1, kept, TILE), f32),
            vmem((tiles + 1, ext, TILE), bf16), vmem((held, ext, WIDTH), bf16), *[wide] * UNROLL, *[flat] * UNROLL,
        ],
    )
    num, den = vmem((tiles_blk, progs, TILE), bf16), vmem((tiles_blk, TILE), f32)
    smoothed = exchange(
        functools.partial(finish_kernel, counts), 2, shape((progs, cells_blk), bf16), (fnum, fden, bnum, bden),
        [
            vmem((blocks, progs, held_blk * WIDTH), f32), vmem((blocks, held_blk, WIDTH), f32),
            vmem((2, tiles_blk, progs, TILE), f32), vmem((2, tiles_blk, TILE), f32),
            vmem((tiles_blk, progs, TILE), f32), den, num, den, num, den, num, den, num, den,
            *dma(6 + 4 * (tiles_blk + 1)),
        ],
    )
    return smoothed[None], row_out, col_out


def solution(mesh):
    in_specs = (
        P("sec", None, "blk"),
        P("sec", None, "blk"),
        P("sec", "blk"),
        P(None, "sec", "blk"),
        P("sec", "blk"),
    )
    out_specs = (P("sec", None, "blk"), P("sec", "blk"), P("sec", "blk"))
    return jax.shard_map(body, mesh=mesh, in_specs=in_specs, out_specs=out_specs, check_vma=False)
```

time: 55.8 us -> 50.1 us (0.90)
  Pallas kernels: 53.6 us -> 46.4 us
  starting transfers between devices: 0 us -> 1.63 us
    pallas_call x3, Pallas kernels: 37 us -> 32.5 us  [exchange(): pl.pallas_call(kernel, out_shape=out_shape, in_specs=[pl.BlockSpec(memory...]
    pallas_call x2, Pallas kernels: 16.6 us -> 13.9 us  [call(): pl.pallas_call(kernel, out_shape=out_shape, in_specs=[pl.BlockSpec(memory...]
    ppermute x0 -> x1, starting transfers between devices: none -> 1.63 us  [body(): lax.ppermute(pack, 'blk', [(source, (source + 2) % blocks) for source in...]
  transfers between devices with their start and end apart: 0 -> 1, of which waited for: 0 -> 0; matrix products, arithmetic and copies ran while one was open for 0% -> 0% of each run, Pallas kernels for 0% -> 23%
where the time goes in v3:
time: 50.1 us; the launch traced here: 50 us
  Pallas kernels  46.4 us (93%)
  starting transfers between devices  1.63 us (3%)
  between operations  1.32 us (3%)
  local copies, waits for them, and re-layouts  0.66 us (1%)
    pallas_call x3, Pallas kernels, exchange(): pl.pallas_call(kernel, out_shape=out_shape, in_specs=[pl.BlockSpec(memory...  32.5 us
    pallas_call x2, Pallas kernels, call(): pl.pallas_call(kernel, out_shape=out_shape, in_specs=[pl.BlockSpec(memory...  13.9 us
    ppermute x1, starting transfers between devices, body(): lax.ppermute(pack, 'blk', [(source, (source + 2) % blocks) for source in...  1.63 us
  transfers between devices with their start and end apart: 1, of which 0 were waited for; matrix products, arithmetic and copies ran while one was open for 0% of the time, Pallas kernels for 23%

profile of v3, /device:TPU:0, one launch (start us, length us, event | category | flops | bytes accessed | tf_op | source)
XLA Modules:
  0.0 50.0 jit_solution(87378679995377567)
XLA Ops:
  1.3 17.9 %shard_map.76 = (bf16[8,128,256]{2,1,0:T(8,128)(2,1)S(1)}, bf16[17,128,512]{2,1,0:T(8,128)(2,1)S(1)}, bf16[17,512,128]{2,1,0:T(8,128)(2,1)S(1)}, f32[4,2,256]{2,...) custom-call(bf16[52,2048]{1,0:T(8,128)(2,1)} %bitcast.4, ...), custom_call_target="tpu_custom_call" | custom-call | tf_op jit(solution)/shard_map/pallas_call | solution.py:639
  19.1 1.6 %collective-permute-start = (bf16[32,5120]{1,0:T(8,128)(2,1)S(1)}, bf16[32,5120]{1,0:T(8,128)(2,1)S(1)}, u32[]{:S(2)}, u32[]{:S(2)}) collective-permute-start(bf16[32,5120]{1,0:T(8,128)(2,1)S(1)} %get-tuple-element.30.near_ref), channel_id=1, source_target_pairs={{0,2},{1,3},{2,0},{3,1},{4,6},{5,7},{6,4},{7,5},{8,10},{9,11},{10,... | collective-permute-start | bytes 983048 | tf_op jit(solution)/shard_map/ppermute | solution.py:709
  20.8 0.0 copy-start
  20.8 7.0 %shard_map.77 = (f32[4,2,256]{2,1,0:T(2,128)S(1)}, bf16[8,256,128]{2,1,0:T(8,128)(2,1)S(1)}, f32[16,512]{1,0:T(8,128)S(1)}) custom-call(s32[8,128]{1,0:T(8,128)S(1)} %get-tuple-element.21.lists_ref, bf16[8,128,256]{2,1,0:T(8,128)(2,1)S(1)} %get-tuple-element.22.xrec_ref, bf16[17,128,512]{2,1,0:T(8,128)(2,1)S(1)} %get-tuple-element.23.y_ref, ...), custom_call_target="tpu_custom_call" | custom-call | tf_op jit(solution)/shard_map/pallas_call | solution.py:650
  27.8 4.3 %shard_map.78 = (f32[24,512]{1,0:T(8,128)S(1)}, f32[4,2,256]{2,1,0:T(2,128)S(1)}) custom-call(f32[4,2,256]{2,1,0:T(2,128)S(1)} %get-tuple-element.27.rp_ref, f32[16,512]{1,0:T(8,128)S(1)} %get-tuple-element.28.cl_ref), custom_call_target="tpu_custom_call" | custom-call | tf_op jit(solution)/shard_map/pallas_call | solution.py:639
  32.2 0.0 collective-permute-done.far_ref
  32.2 0.0 copy-done
  32.2 6.8 %shard_map.79 = (f32[4,32,512]{2,1,0:T(8,128)S(1)}, f32[4,2,256]{2,1,0:T(2,128)S(1)}, f32[4,4,32,512]{3,2,1,0:T(8,128)S(1)}, f32[4,4,512]{2,1,0:T(4,128)S(1)}, f32[1,2048]{1,0:T(1,128)}, /*index=5*/f32[1,2048]{1,0:T(1,128)}) custom-call(s32[8,128]{1,0:T(8,128)S(1)} %get-tuple-element.21.lists_ref, bf16[8,256,128]{2,1,0:T(8,128)(2,1)S(1)} %get-tuple-element.26.xt_ref, ...), custom_call_target="tpu_custom_call" | custom-call | tf_op jit(solution)/shard_map/pallas_call | solution.py:650
  39.0 10.3 %shard_map.80 = bf16[32,2048]{1,0:T(8,128)(2,1)S(1)} custom-call(f32[4,32,512]{2,1,0:T(8,128)S(1)} %get-tuple-element.33.fnum_ref, f32[4,2,256]{2,1,0:T(2,128)S(1)} %get-tuple-element.34.fden_ref, f32[4,4,32,512]{3,2,1,0:T(8,128)S(1)} %get-tuple-element.35.bnum_ref, f32[4,4,512]{2,1,0:T(4,128)S(1)} %get-tuple-element.36.bden_ref), custom_call_target="tpu_custom_call" | custom-call | tf_op jit(solution)/shard_map/pallas_call | solution.py:639
  49.3 0.7 %copy.10 = bf16[1,32,2048]{2,1,0:T(8,128)(2,1)} copy(bf16[1,32,2048]{2,1,0:T(8,128)(2,1)S(1)} %bitcast.3) | data formatting | bytes 262144
Async XLA Ops:
  19.1 13.0 %collective-permute-start = (bf16[32,5120]{1,0:T(8,128)(2,1)S(1)}, bf16[32,5120]{1,0:T(8,128)(2,1)S(1)}, u32[]{:S(2)}, u32[]{:S(2)}) collective-permute-start(bf16[32,5120]{1,0:T(8,128)(2,1)S(1)} %get-tuple-element.30.near_ref), channel_id=1, source_target_pairs={{0,2},{1,3},{2,0},{3,1},{4,6},{5,7},{6,4},{7,5},{8,10},{9,11},{10,... | collective-permute-start | bytes 983048 | tf_op jit(solution)/shard_map/ppermute | solution.py:709
  20.8 11.4 %copy-start = (bf16[1,2048]{1,0:T(2,128)(2,1)S(1)}, bf16[1,2048]{1,0:T(2,128)(2,1)}, u32[]{:S(2)}) copy-start(bf16[1,2048]{1,0:T(2,128)(2,1)} %pot_ref.3) | copy-start | bytes 12292

commit v4 on v3

--- a/solution.py
+++ b/solution.py
@@ -13,6 +13,7 @@
 LOG2E = math.log2(math.e)
 NEG = -1e30
 UNROLL = 4
+SLOTS = 2
 SPLITS = 2
 WIDTH = TILE // SPLITS
 LANES = 128
@@ -93,6 +94,7 @@
 
 
 FEAT_CHUNKS = 4
+LAG = 3
 PARTS = 1
 
 
@@ -142,10 +144,6 @@
     piece = held_blk * WIDTH
     has_to, has_from = sec > 0, sec < n_sec - 1
     core, across, corner = mates = mates_of(blk, blocks)
-    me = blk % 2
-    mine_at = pl.multiple_of(me * cells_blk, LANES)
-    beside_at = pl.multiple_of(SPLITS * cells_blk + me * piece, LANES)
-    own_at = pl.multiple_of(me * piece, LANES)
 
     def prog_piece(owner, place):
         return prog_ref.at[:, pl.ds(pl.multiple_of(lane_of(owner, place, blocks), WIDTH), WIDTH)]
@@ -155,8 +153,11 @@
         start = pl.multiple_of(lane_of(blk, place, blocks), WIDTH)
         moves.append((x_ref.at[:, pl.ds(start, WIDTH)], own_x.at[blk, place]))
     for place in range(held_blk):
-        moves.append((prog_piece(blk, place), pown_ref.at[:, pl.ds(own_at + place * WIDTH, WIDTH)]))
-        moves.append((prog_piece(across, place), pack_ref.at[:, pl.ds(beside_at + place * WIDTH, WIDTH)]))
+        for owner, buffer, start in (
+            (blk, pown_ref, 0), (core, pown_ref, piece), (across, pack_ref, cells_blk), (corner, pack_ref, cells_blk + piece)
+        ):
+            start += place * WIDTH
+            moves.append((prog_piece(owner, place), buffer.at[:, start : start + WIDTH]))
     locals_ = [pltpu.make_async_copy(src, dst, local_sem.at[n]) for n, (src, dst) in enumerate(moves)]
     for copy in locals_:
         copy.start()
@@ -171,19 +172,14 @@
     def first(c):
         start, size = chunks[c]
         return send(
-            x_ref.at[:, start : start + size], xs.at[blk, :, start : start + size], sems, 4 * c, sec - 1, blk
+            x_ref.at[:, start : start + size], xs.at[blk, c], sems, 4 * c, sec - 1, blk
         )
 
     def first_programs():
-        return send(prog_ref, pack_ref.at[:, pl.ds(mine_at, cells_blk)], sems, last, sec - 1, blk)
-
-    def share_programs():
-        slot = pack_ref.at[:, pl.ds(mine_at, cells_blk)]
-        return send(slot, slot, sems, last + 1, sec, core)
+        return send(prog_ref, pack_ref.at[:, 0:cells_blk], sems, last, sec - 1, blk)
 
     def share(c, kind):
-        start, size = chunks[c]
-        slot = xs.at[across if kind == 2 else blk, :, start : start + size]
+        slot = xs.at[across if kind == 2 else blk, c]
         return send(slot, slot, sems, 4 * c + 1 + kind, sec, across if kind == 0 else core)
 
     def to_mate(k):
@@ -195,14 +191,6 @@
         per = len(copies)
         return [send(src, dst, mate_sems, per * k + n, sec, mate) for n, (src, dst) in enumerate(copies)]
 
-    def pieces_to_core():
-        base = 3 * (held_blk + 3)
-        copies = []
-        for place in range(held_blk):
-            copies.append((prog_piece(core, place), pown_ref.at[:, pl.ds(own_at + place * WIDTH, WIDTH)]))
-            copies.append((prog_piece(corner, place), pack_ref.at[:, pl.ds(beside_at + place * WIDTH, WIDTH)]))
-        return [send(src, dst, mate_sems, base + n, sec, core) for n, (src, dst) in enumerate(copies)]
-
     @pl.when(has_to)
     def _():
         for c in range(len(chunks)):
@@ -213,9 +201,6 @@
     for n in range(len(to_mates[0])):
         for k in (1, 2, 0):
             to_mates[k][n].start()
-    to_core = pieces_to_core()
-    for copy in to_core:
-        copy.start()
 
     xbuild[...] = jnp.zeros_like(xbuild)
     xbuild[aux:depth, :] = rows_of([1.0] * 3, WIDTH)
@@ -243,7 +228,7 @@
         begin, size = chunks[c]
         for start in range(begin, begin + size, TILE):
             tile = owner * tiles_blk + start // TILE
-            cells = xs[owner, :, start : start + TILE].astype(jnp.float32)
+            cells = xs[owner, c, :, start - begin : start - begin + TILE].astype(jnp.float32)
             pot = pots[owner, :, start : start + TILE].astype(jnp.float32)
             bias = pot * (LOG2E / EPSILON) - sum_squares(cells) * (gain * 0.5)
             ybuild[0:feat, :] = cells
@@ -260,36 +245,31 @@
 
     @pl.when(has_from)
     def _():
-        for turn in range(len(chunks) + 2):
+        for turn in range(len(chunks) + LAG + 1):
             if turn < len(chunks):
                 first(turn).wait_recv()
                 share(turn, 0).start()
                 share(turn, 1).start()
                 build_next(blk, turn)
-            if 0 <= turn - 1 < len(chunks):
-                share(turn - 1, 0).wait_recv()
-                share(turn - 1, 2).start()
-                build_next(across, turn - 1)
-                share(turn - 1, 1).wait_recv()
-                build_next(core, turn - 1)
-            if turn == len(chunks):
-                first_programs().wait_recv()
-                share_programs().start()
-            if 0 <= turn - 2 < len(chunks):
-                share(turn - 2, 2).wait_recv()
-                build_next(corner, turn - 2)
-        share_programs().wait_recv()
+            if 0 <= turn - LAG < len(chunks):
+                share(turn - LAG, 0).wait_recv()
+                share(turn - LAG, 2).start()
+                share(turn - LAG, 1).wait_recv()
+                build_next(core, turn - LAG)
+                build_next(across, turn - LAG)
+            if 0 <= turn - LAG - 1 < len(chunks):
+                share(turn - LAG - 1, 2).wait_recv()
+                build_next(corner, turn - LAG - 1)
+        first_programs().wait_recv()
 
     @pl.when(jnp.logical_not(has_from))
     def _():
-        pack_ref[:, 0 : SPLITS * cells_blk] = jnp.zeros((pack_ref.shape[0], SPLITS * cells_blk), jnp.bfloat16)
+        pack_ref[:, 0:cells_blk] = jnp.zeros((pack_ref.shape[0], cells_blk), jnp.bfloat16)
 
     for k, mate in enumerate(mates):
         for copy in to_mates[k][3:]:
             copy.wait_recv()
         build_own(mate)
-    for copy in to_core:
-        copy.wait_recv()
 
     @pl.when(has_to)
     def _():
@@ -302,17 +282,14 @@
         for c in range(len(chunks)):
             for kind in range(3):
                 share(c, kind).wait_send()
-        share_programs().wait_send()
 
     for k in range(3):
         for copy in to_mates[k]:
             copy.wait_send()
-    for copy in to_core:
-        copy.wait_send()
-
-
-def rounds_of(lists_ref):
-    return (lists_ref[2, 0] + UNROLL - 1) // UNROLL
+
+
+def rounds_of(lists_ref, unroll):
+    return (lists_ref[2, 0] + unroll - 1) // unroll
 
 
 def stats_kernel(dims, lists_ref, xrec_ref, y_ref, yt_ref, sq_ref, rp_ref, xt_out, cl_ref,
@@ -325,7 +302,7 @@
     depth = depth_of(feat)
     aux = depth - 8
     at_end = lax.axis_index("sec") == lax.axis_size("sec") - 1
-    rounds = rounds_of(lists_ref)
+    rounds = rounds_of(lists_ref, UNROLL)
     for ref in (top_row, top_col):
         ref[...] = jnp.full_like(ref, NEG)
     for ref in (sum_row, sum_col):
@@ -397,34 +374,49 @@
         cl_ref[col : col + 1, :] = jnp.where(total > 0.0, top + jnp.log2(total), NEG)
 
 
-def merge_kernel(counts, rp_ref, cl_ref, level_ref, home_ref, parts, send_sem, recv_sem):
+def merge_kernel(counts, rp_ref, cl_ref, pack_ref, pown_ref, far_ref, level_ref, home_ref, extra_ref,
+                 parts, send_sem, recv_sem):
     n_sec, blocks = counts
     sec, blk = lax.axis_index("sec"), lax.axis_index("blk")
     tiles = cl_ref.shape[0]
-    mates = mates_of(blk, blocks)
+    core, across, corner = mates = mates_of(blk, blocks)
     sems = (send_sem, recv_sem)
     greet([(sec >= 0, sec, mate) for mate in mates])
     copies = []
     for k, mate in enumerate(mates):
         copies.append(send(cl_ref, parts.at[blk], sems, 2 * k, sec, mate))
         copies.append(send(rp_ref.at[mate], home_ref.at[blk], sems, 2 * k + 1, sec, mate))
+    piece = pown_ref.shape[1] // 2
+    cells = pack_ref.shape[1] - 2 * piece
+    beside = [
+        (pown_ref, piece, piece, 2 * cells), (far_ref, cells + piece, piece, 2 * cells + piece),
+        (pack_ref, 0, cells, 0), (far_ref, 0, cells, cells),
+    ]
+    for n, (ref, start, size, place) in enumerate(beside):
+        copies.append(
+            send(ref.at[:, start : start + size], extra_ref.at[:, place : place + size], sems, 2 * len(mates) + n, sec, core)
+        )
     for k in (1, 2, 0):
         for copy in copies[2 * k : 2 * k + 2]:
             copy.start()
+    for copy in copies[2 * len(mates) :]:
+        copy.start()
     parts[blk] = cl_ref[...]
     home_ref[blk] = rp_ref[blk]
     level_ref[tiles:, :] = jnp.zeros((level_ref.shape[0] - tiles, TILE), jnp.float32)
-    for copy in copies:
+    for copy in copies[: 2 * len(mates)]:
         copy.wait_recv()
     levels = [parts[n] for n in range(blocks)]
     top = functools.reduce(jnp.maximum, levels)
     total = functools.reduce(jnp.add, [jnp.exp2(level - top) for level in levels])
     level_ref[0:tiles, :] = top + jnp.log2(total)
+    for copy in copies[2 * len(mates) :]:
+        copy.wait_recv()
     for copy in copies:
         copy.wait_send()
 
 
-def plan_kernel(dims, lists_ref, xt_ref, y_ref, level_ref, near_ref, pown_ref, far_ref, pot_ref, home_ref,
+def plan_kernel(dims, lists_ref, xt_ref, y_ref, level_ref, pack_ref, pown_ref, far_ref, extra_ref, pot_ref, home_ref,
                 fnum_ref, fden_ref, bnum_ref, bden_ref, rows_ref, cols_ref,
                 acc_row, acc_col, ext_next_ref, ext_own_ref, *ready):
     feat, blocks, tiles_blk = dims
@@ -437,32 +429,33 @@
     kept = acc_row.shape[1]
     at_end = lax.axis_index("sec") == lax.axis_size("sec") - 1
     blk = lax.axis_index("blk")
-    side = blk // SPLITS
-    rounds = rounds_of(lists_ref)
-    scores, plans = ready[:UNROLL], ready[UNROLL:]
+    rounds = rounds_of(lists_ref, SLOTS)
+    scores, plans = ready[:SLOTS], ready[SLOTS:]
 
     def make(at, place):
         scores[place][...] = jnp.dot(
             xt_ref[lists_ref[0, at]], y_ref[lists_ref[1, at]], preferred_element_type=jnp.float32
         )
 
-    for n in range(UNROLL):
-        make(UNROLL + n, n)
-        plans[n][...] = jnp.zeros_like(plans[n])
+    make(UNROLL, 0)
+    plans[1][...] = jnp.zeros_like(plans[1])
     acc_row[...] = jnp.zeros_like(acc_row)
     acc_col[...] = jnp.zeros_like(acc_col)
     ext_next_ref[tiles] = jnp.zeros(ext_next_ref.shape[1:], jnp.bfloat16)
-    for group, nums, owns, shift in ((side, near_ref, pown_ref, 0), (1 - side, far_ref, far_ref, SPLITS * cells_blk)):
-        for n in range(SPLITS):
-            owner = group * SPLITS + n
-            for tile in range(tiles_blk):
-                start = n * cells_blk + tile * TILE
-                ext_next_ref[owner * tiles_blk + tile, 0:progs, :] = nums[:, start : start + TILE]
-                ext_next_ref[owner * tiles_blk + tile, progs:, :] = ext_tail(progs, TILE)
-            for place in range(held_blk):
-                start = shift + n * piece + place * WIDTH
-                ext_own_ref[owner * held_blk + place, 0:progs, :] = owns[:, start : start + WIDTH]
-                ext_own_ref[owner * held_blk + place, progs:, :] = ext_tail(progs, WIDTH)
+    core, across, corner = mates_of(blk, blocks)
+    sources = (
+        (blk, pack_ref, 0, pown_ref, 0), (core, extra_ref, 0, extra_ref, 2 * cells_blk),
+        (across, far_ref, 0, far_ref, cells_blk), (corner, extra_ref, cells_blk, extra_ref, 2 * cells_blk + piece),
+    )
+    for owner, nums, begin, owns, shift in sources:
+        for tile in range(tiles_blk):
+            start = begin + tile * TILE
+            ext_next_ref[owner * tiles_blk + tile, 0:progs, :] = nums[:, start : start + TILE]
+            ext_next_ref[owner * tiles_blk + tile, progs:, :] = ext_tail(progs, TILE)
+        for place in range(held_blk):
+            start = shift + place * WIDTH
+            ext_own_ref[owner * held_blk + place, 0:progs, :] = owns[:, start : start + WIDTH]
+            ext_own_ref[owner * held_blk + place, progs:, :] = ext_tail(progs, WIDTH)
     for owner in range(blocks):
         for place in range(held_blk):
             start = lane_of(owner, place, blocks)
@@ -486,16 +479,15 @@
         acc_col[col] += jnp.dot(ext_own_ref[row], plan, preferred_element_type=jnp.float32)[0:kept]
 
     def step(index, carry):
-        for n in range(UNROLL):
-            at = index * UNROLL + UNROLL + n
-            gather(at - UNROLL, n)
+        for n in range(SLOTS):
+            at = index * SLOTS + UNROLL + n
+            make(at + 1, (n + 1) % SLOTS)
+            gather(at - 1, (n + 1) % SLOTS)
             weigh(at, n)
-            make(at + UNROLL, n)
         return carry
 
     lax.fori_loop(0, rounds, step, 0)
-    for n in range(UNROLL):
-        gather(rounds * UNROLL + n, n)
+    gather(rounds * SLOTS + UNROLL - 1, SLOTS - 1)
     for row in range(held):
         owner, place = row // held_blk, row % held_blk
         fnum_ref[owner, :, place * WIDTH : (place + 1) * WIDTH] = acc_row[row, 0:progs, :]
@@ -676,8 +668,8 @@
 
     piece = held_blk * WIDTH
     kept = -(-(progs + 1) // 8) * 8
-    mate_copies = (blocks - 1) * (held_blk + 3) + 2 * held_blk
-    packed = SPLITS * (cells_blk + piece)
+    mate_copies = (blocks - 1) * (held_blk + 3)
+    packed = cells_blk + 2 * piece
     spaced = [
         pltpu.with_memory_space_constraint(part, pltpu.HBM)
         for part in (features[0], programs[0], column_pot, tile_pairs)
@@ -690,19 +682,19 @@
             shape((tiles + 1, TILE, 2 * depth), bf16),
             shape((blocks, held_blk, WIDTH), f32),
             shape((progs, packed), bf16),
-            shape((progs, SPLITS * piece), bf16),
+            shape((progs, 2 * piece), bf16),
             shape((8, lists_width(blocks, most)), i32),
         ),
         (*spaced, pair_counts),
         [
-            vmem((blocks, feat, cells_blk), bf16),
+            vmem((blocks, FEAT_CHUNKS, feat, cells_blk // FEAT_CHUNKS), bf16),
             vmem((blocks, held_blk, feat, WIDTH), bf16),
             vmem((blocks, 1, cells_blk), bf16),
             vmem((blocks, 2, 1, most), i32),
             vmem((blocks, 1, 1), i32),
             vmem((2 * depth, WIDTH), f32),
             vmem((2 * depth, TILE), f32),
-            *dma(4 * FEAT_CHUNKS + 2), *dma(mate_copies), pltpu.SemaphoreType.DMA((3 + 3 * held_blk,)),
+            *dma(4 * FEAT_CHUNKS + 1), *dma(mate_copies), pltpu.SemaphoreType.DMA((3 + 5 * held_blk,)),
         ],
         pltpu.HBM,
     )
@@ -719,9 +711,10 @@
             vmem((UNROLL, 8, WIDTH), f32), vmem((UNROLL, 8, TILE), f32), *[tall] * UNROLL, *[wide] * UNROLL,
         ],
     )
-    level, home = exchange(
-        functools.partial(merge_kernel, counts), 1, (shape((tiles + 8, TILE), f32), pots), (rp, cl),
-        [vmem((blocks, tiles, TILE), f32), *dma(2 * (blocks - 1))],
+    level, home, extra = exchange(
+        functools.partial(merge_kernel, counts), 1,
+        (shape((tiles + 8, TILE), f32), pots, shape((progs, 2 * (cells_blk + piece)), bf16)), (rp, cl, pack, pown, far),
+        [vmem((blocks, tiles, TILE), f32), *dma(2 * (blocks - 1) + 4)],
     )
     line = shape((1, cells_blk), f32)
     flat = vmem((WIDTH, TILE), bf16)
@@ -731,10 +724,10 @@
             shape((blocks, progs, held_blk * WIDTH), f32), pots,
             shape((blocks, tiles_blk, progs, TILE), f32), shape((blocks, tiles_blk, TILE), f32), line, line,
         ),
-        (lists, xt, y, level, pack, pown, far, column_pot, home),
+        (lists, xt, y, level, pack, pown, far, extra, column_pot, home),
         [
             vmem((held, kept, WIDTH), f32), vmem((tiles + 1, kept, TILE), f32),
-            vmem((tiles + 1, ext, TILE), bf16), vmem((held, ext, WIDTH), bf16), *[wide] * UNROLL, *[flat] * UNROLL,
+            vmem((tiles + 1, ext, TILE), bf16), vmem((held, ext, WIDTH), bf16), *[wide] * SLOTS, *[flat] * SLOTS,
         ],
     )
     num, den = vmem((tiles_blk, progs, TILE), bf16), vmem((tiles_blk, TILE), f32)

time: 50.1 us -> 48.6 us (0.970)
  starting transfers between devices: 1.63 us -> 0.58 us
  Pallas kernels: 46.4 us -> 45.7 us
    ppermute x1, starting transfers between devices: 1.63 us -> 0.58 us  [body(): lax.ppermute(pack, 'blk', [(source, (source + 2) % blocks) for source in...]
    pallas_call x3, Pallas kernels: 32.5 us -> 31.9 us  [exchange(): pl.pallas_call(kernel, out_shape=out_shape, in_specs=[pl.BlockSpec(memory...]
  transfers between devices with their start and end apart: 1 -> 1, of which waited for: 0 -> 0; matrix products, arithmetic and copies ran while one was open for 0% -> 0% of each run, Pallas kernels for 23% -> 15%
where the time goes in v4:
time: 48.6 us; the launch traced here: 48.3 us
  Pallas kernels  45.7 us (94%)
  between operations  1.32 us (3%)
  local copies, waits for them, and re-layouts  0.66 us (1%)
  starting transfers between devices  0.58 us (1%)
    pallas_call x3, Pallas kernels, exchange(): pl.pallas_call(kernel, out_shape=out_shape, in_specs=[pl.BlockSpec(memory...  31.9 us
    pallas_call x2, Pallas kernels, call(): pl.pallas_call(kernel, out_shape=out_shape, in_specs=[pl.BlockSpec(memory...  13.8 us
  transfers between devices with their start and end apart: 1, of which 0 were waited for; matrix products, arithmetic and copies ran while one was open for 0% of the time, Pallas kernels for 15%

profile of v4, /device:TPU:0, one launch (start us, length us, event | category | flops | bytes accessed | tf_op | source)
XLA Modules:
  0.0 48.3 jit_solution(4018174915422496311)
XLA Ops:
  1.3 16.6 %shard_map.76 = (bf16[8,128,256]{2,1,0:T(8,128)(2,1)S(1)}, bf16[17,128,512]{2,1,0:T(8,128)(2,1)S(1)}, bf16[17,512,128]{2,1,0:T(8,128)(2,1)S(1)}, f32[4,2,256]{2,...) custom-call(bf16[52,2048]{1,0:T(8,128)(2,1)} %bitcast.4, ...), custom_call_target="tpu_custom_call" | custom-call | tf_op jit(solution)/shard_map/pallas_call | solution.py:631
  17.8 0.6 %collective-permute-start = (bf16[32,3072]{1,0:T(8,128)(2,1)S(1)}, bf16[32,3072]{1,0:T(8,128)(2,1)S(1)}, u32[]{:S(2)}, u32[]{:S(2)}) collective-permute-start(bf16[32,3072]{1,0:T(8,128)(2,1)S(1)} %get-tuple-element.30.pack_ref), channel_id=1, source_target_pairs={{0,2},{1,3},{2,0},{3,1},{4,6},{5,7},{6,4},{7,5},{8,10},{9,11},{10,... | collective-permute-start | bytes 589832 | tf_op jit(solution)/shard_map/ppermute | solution.py:701
  18.4 0.0 copy-start
  18.4 7.1 %shard_map.77 = (f32[4,2,256]{2,1,0:T(2,128)S(1)}, bf16[8,256,128]{2,1,0:T(8,128)(2,1)S(1)}, f32[16,512]{1,0:T(8,128)S(1)}) custom-call(s32[8,128]{1,0:T(8,128)S(1)} %get-tuple-element.22.lists_ref, bf16[8,128,256]{2,1,0:T(8,128)(2,1)S(1)} %get-tuple-element.23.xrec_ref, bf16[17,128,512]{2,1,0:T(8,128)(2,1)S(1)} %get-tuple-element.24.y_ref, ...), custom_call_target="tpu_custom_call" | custom-call | tf_op jit(solution)/shard_map/pallas_call | solution.py:642
  25.5 0.0 collective-permute-done.far_ref
  25.5 4.4 %shard_map.78 = (f32[24,512]{1,0:T(8,128)S(1)}, f32[4,2,256]{2,1,0:T(2,128)S(1)}, bf16[32,5120]{1,0:T(8,128)(2,1)S(1)}) custom-call(f32[4,2,256]{2,1,0:T(2,128)S(1)} %get-tuple-element.28.rp_ref, f32[16,512]{1,0:T(8,128)S(1)} %get-tuple-element.29.cl_ref, bf16[32,3072]{1,0:T(8,128)(2,1)S(1)} %get-tuple-element.30.pack_ref, ...), custom_call_target="tpu_custom_call" | custom-call | tf_op jit(solution)/shard_map/pallas_call | solution.py:631
  29.9 0.0 copy-done
  29.9 6.7 %shard_map.79 = (f32[4,32,512]{2,1,0:T(8,128)S(1)}, f32[4,2,256]{2,1,0:T(2,128)S(1)}, f32[4,4,32,512]{3,2,1,0:T(8,128)S(1)}, f32[4,4,512]{2,1,0:T(4,128)S(1)}, f32[1,2048]{1,0:T(1,128)}, /*index=5*/f32[1,2048]{1,0:T(1,128)}) custom-call(s32[8,128]{1,0:T(8,128)S(1)} %get-tuple-element.22.lists_ref, bf16[8,256,128]{2,1,0:T(8,128)(2,1)S(1)} %get-tuple-element.27.xt_ref, ...), custom_call_target="tpu_custom_call" | custom-call | tf_op jit(solution)/shard_map/pallas_call | solution.py:642
  36.6 11.0 %shard_map.80 = bf16[32,2048]{1,0:T(8,128)(2,1)S(1)} custom-call(f32[4,32,512]{2,1,0:T(8,128)S(1)} %get-tuple-element.35.fnum_ref, f32[4,2,256]{2,1,0:T(2,128)S(1)} %get-tuple-element.36.fden_ref, f32[4,4,32,512]{3,2,1,0:T(8,128)S(1)} %get-tuple-element.37.bnum_ref, f32[4,4,512]{2,1,0:T(4,128)S(1)} %get-tuple-element.38.bden_ref), custom_call_target="tpu_custom_call" | custom-call | tf_op jit(solution)/shard_map/pallas_call | solution.py:631
  47.6 0.7 %copy.10 = bf16[1,32,2048]{2,1,0:T(8,128)(2,1)} copy(bf16[1,32,2048]{2,1,0:T(8,128)(2,1)S(1)} %bitcast.3) | data formatting | bytes 262144
Async XLA Ops:
  17.8 7.6 %collective-permute-start = (bf16[32,3072]{1,0:T(8,128)(2,1)S(1)}, bf16[32,3072]{1,0:T(8,128)(2,1)S(1)}, u32[]{:S(2)}, u32[]{:S(2)}) collective-permute-start(bf16[32,3072]{1,0:T(8,128)(2,1)S(1)} %get-tuple-element.30.pack_ref), channel_id=1, source_target_pairs={{0,2},{1,3},{2,0},{3,1},{4,6},{5,7},{6,4},{7,5},{8,10},{9,11},{10,... | collective-permute-start | bytes 589832 | tf_op jit(solution)/shard_map/ppermute | solution.py:701
  18.4 11.5 %copy-start = (bf16[1,2048]{1,0:T(2,128)(2,1)S(1)}, bf16[1,2048]{1,0:T(2,128)(2,1)}, u32[]{:S(2)}) copy-start(bf16[1,2048]{1,0:T(2,128)(2,1)} %pot_ref.3) | copy-start | bytes 12292

commit v5 on v4

--- a/solution.py
+++ b/solution.py
@@ -195,6 +195,9 @@
     def _():
         for c in range(len(chunks)):
             first(c).start()
+
+    @pl.when(jnp.logical_and(has_to, jnp.logical_not(has_from)))
+    def _():
         first_programs().start()
 
     to_mates = [to_mate(k) for k in range(3)]
@@ -250,6 +253,12 @@
                 first(turn).wait_recv()
                 share(turn, 0).start()
                 share(turn, 1).start()
+                if turn == 1:
+
+                    @pl.when(has_to)
+                    def _():
+                        first_programs().start()
+
                 build_next(blk, turn)
             if 0 <= turn - LAG < len(chunks):
                 share(turn - LAG, 0).wait_recv()

time: 48.6 us -> 49.2 us (1.012)
    pallas_call x3, Pallas kernels: 31.9 us -> 32.6 us  [exchange(): pl.pallas_call(kernel, out_shape=out_shape, in_specs=[pl.BlockSpec(memory...]
where the time goes in v5:
time: 49.2 us; the launch traced here: 48.4 us
  Pallas kernels  45.9 us (93%)
  between operations  1.32 us (3%)
  local copies, waits for them, and re-layouts  0.66 us (1%)
  starting transfers between devices  0.56 us (1%)
    pallas_call x3, Pallas kernels, exchange(): pl.pallas_call(kernel, out_shape=out_shape, in_specs=[pl.BlockSpec(memory...  32.6 us
    pallas_call x2, Pallas kernels, call(): pl.pallas_call(kernel, out_shape=out_shape, in_specs=[pl.BlockSpec(memory...  13.3 us
  transfers between devices with their start and end apart: 1, of which 0 were waited for; matrix products, arithmetic and copies ran while one was open for 0% of the time, Pallas kernels for 15%

profile of v5, /device:TPU:0, one launch (start us, length us, event | category | flops | bytes accessed | tf_op | source)
XLA Modules:
  0.0 48.4 jit_solution(7925083101887793025)
XLA Ops:
  1.3 16.3 %shard_map.76 = (bf16[8,128,256]{2,1,0:T(8,128)(2,1)S(1)}, bf16[17,128,512]{2,1,0:T(8,128)(2,1)S(1)}, bf16[17,512,128]{2,1,0:T(8,128)(2,1)S(1)}, f32[4,2,256]{2,...) custom-call(bf16[52,2048]{1,0:T(8,128)(2,1)} %bitcast.4, ...), custom_call_target="tpu_custom_call" | custom-call | tf_op jit(solution)/shard_map/pallas_call | solution.py:640
  17.6 0.6 %collective-permute-start = (bf16[32,3072]{1,0:T(8,128)(2,1)S(1)}, bf16[32,3072]{1,0:T(8,128)(2,1)S(1)}, u32[]{:S(2)}, u32[]{:S(2)}) collective-permute-start(bf16[32,3072]{1,0:T(8,128)(2,1)S(1)} %get-tuple-element.30.pack_ref), channel_id=1, source_target_pairs={{0,2},{1,3},{2,0},{3,1},{4,6},{5,7},{6,4},{7,5},{8,10},{9,11},{10,... | collective-permute-start | bytes 589832 | tf_op jit(solution)/shard_map/ppermute | solution.py:710
  18.2 0.0 copy-start
  18.2 7.1 %shard_map.77 = (f32[4,2,256]{2,1,0:T(2,128)S(1)}, bf16[8,256,128]{2,1,0:T(8,128)(2,1)S(1)}, f32[16,512]{1,0:T(8,128)S(1)}) custom-call(s32[8,128]{1,0:T(8,128)S(1)} %get-tuple-element.22.lists_ref, bf16[8,128,256]{2,1,0:T(8,128)(2,1)S(1)} %get-tuple-element.23.xrec_ref, bf16[17,128,512]{2,1,0:T(8,128)(2,1)S(1)} %get-tuple-element.24.y_ref, ...), custom_call_target="tpu_custom_call" | custom-call | tf_op jit(solution)/shard_map/pallas_call | solution.py:651
  25.3 0.0 collective-permute-done.far_ref
  25.3 4.4 %shard_map.78 = (f32[24,512]{1,0:T(8,128)S(1)}, f32[4,2,256]{2,1,0:T(2,128)S(1)}, bf16[32,5120]{1,0:T(8,128)(2,1)S(1)}) custom-call(f32[4,2,256]{2,1,0:T(2,128)S(1)} %get-tuple-element.28.rp_ref, f32[16,512]{1,0:T(8,128)S(1)} %get-tuple-element.29.cl_ref, bf16[32,3072]{1,0:T(8,128)(2,1)S(1)} %get-tuple-element.30.pack_ref, ...), custom_call_target="tpu_custom_call" | custom-call | tf_op jit(solution)/shard_map/pallas_call | solution.py:640
  29.7 0.0 copy-done
  29.7 6.3 %shard_map.79 = (f32[4,32,512]{2,1,0:T(8,128)S(1)}, f32[4,2,256]{2,1,0:T(2,128)S(1)}, f32[4,4,32,512]{3,2,1,0:T(8,128)S(1)}, f32[4,4,512]{2,1,0:T(4,128)S(1)}, f32[1,2048]{1,0:T(1,128)}, /*index=5*/f32[1,2048]{1,0:T(1,128)}) custom-call(s32[8,128]{1,0:T(8,128)S(1)} %get-tuple-element.22.lists_ref, bf16[8,256,128]{2,1,0:T(8,128)(2,1)S(1)} %get-tuple-element.27.xt_ref, ...), custom_call_target="tpu_custom_call" | custom-call | tf_op jit(solution)/shard_map/pallas_call | solution.py:651
  36.0 11.8 %shard_map.80 = bf16[32,2048]{1,0:T(8,128)(2,1)S(1)} custom-call(f32[4,32,512]{2,1,0:T(8,128)S(1)} %get-tuple-element.35.fnum_ref, f32[4,2,256]{2,1,0:T(2,128)S(1)} %get-tuple-element.36.fden_ref, f32[4,4,32,512]{3,2,1,0:T(8,128)S(1)} %get-tuple-element.37.bnum_ref, f32[4,4,512]{2,1,0:T(4,128)S(1)} %get-tuple-element.38.bden_ref), custom_call_target="tpu_custom_call" | custom-call | tf_op jit(solution)/shard_map/pallas_call | solution.py:640
  47.8 0.7 %copy.10 = bf16[1,32,2048]{2,1,0:T(8,128)(2,1)} copy(bf16[1,32,2048]{2,1,0:T(8,128)(2,1)S(1)} %bitcast.3) | data formatting | bytes 262144
Async XLA Ops:
  17.6 7.6 %collective-permute-start = (bf16[32,3072]{1,0:T(8,128)(2,1)S(1)}, bf16[32,3072]{1,0:T(8,128)(2,1)S(1)}, u32[]{:S(2)}, u32[]{:S(2)}) collective-permute-start(bf16[32,3072]{1,0:T(8,128)(2,1)S(1)} %get-tuple-element.30.pack_ref), channel_id=1, source_target_pairs={{0,2},{1,3},{2,0},{3,1},{4,6},{5,7},{6,4},{7,5},{8,10},{9,11},{10,... | collective-permute-start | bytes 589832 | tf_op jit(solution)/shard_map/ppermute | solution.py:710
  18.2 11.5 %copy-start = (bf16[1,2048]{1,0:T(2,128)(2,1)S(1)}, bf16[1,2048]{1,0:T(2,128)(2,1)}, u32[]{:S(2)}) copy-start(bf16[1,2048]{1,0:T(2,128)(2,1)} %pot_ref.3) | copy-start | bytes 12292
